TPU v7x, 32 devices: a whole 2x2x4 slice. The times are simulated.
32 devices in a mesh: node: 8 (over z, x), query: 4 (over y, core).
Axes of the slice: x: 2, y: 2, z: 4, core: 2. Of those that a mesh axis runs over, the one named last changes fastest.
Arguments:
- entity_state: bfloat16 [8192, 2048], P('node', 'query'), may hold values from -6 to 6
- edge_tiles: int32 [128, 3, 512], P('node'), may hold values from 0 to 4095, as said below
- query_head: int32 [64], P('query'), may hold values from 0 to 8191
- query_relation: int32 [64], P('query'), may hold values from 0 to 821
- query_table: float32 [822, 32], replicated, may hold values from -6 to 6
- rel_vectors: float32 [2, 822, 32], replicated, may hold values from -1.8 to 1.8
- mix_weight: float32 [2, 32, 32], replicated, may hold values from -1 to 1
- mix_bias: float32 [2, 32], replicated, may hold values from -3 to 3
- cotangent: bfloat16 [8192, 2048], P('node', 'query'), may hold values from -6 to 6
Outputs:
- final_state: bfloat16 [8192, 2048], P('node', 'query')
- weight_grads: float32 [2, 32, 32], replicated
- bias_grads: float32 [2, 32], replicated
Inputs may be any that keep to these rules, and one draw needn't show every extreme that they name: edge_tiles[t,0,:] lies in 0 to 4095, edge_tiles[t,1,:] in 0 to 63, edge_tiles[t,2,:] in 0 to 821.
All inputs are finite; a program needn't handle non-finite values.
Results may differ from a plain program's by a relative error of at most 0.0056.
Values may be sent and summed in bfloat16 or wider, within the bound.
No kernel may reach another device: no remote copies, remote signals or barrier semaphores. Data moves between devices by JAX's collectives and lax.ppermute only.
A program may use at most 192 MiB of HBM per device.

v0:
```python
import jax
import jax.numpy as jnp
from jax import lax
from jax.sharding import PartitionSpec as P

DIM = 32


def with_halo(block, sides, width):
    for axis, dim in sides:
        count = lax.axis_size(axis)
        forward = [(i, i + 1) for i in range(count - 1)]
        forward.append((count - 1, 0))
        backward = [(target, source) for source, target in forward]
        low = lax.ppermute(
            lax.slice_in_dim(block, block.shape[dim] - width, None, axis=dim), axis, forward
        )
        high = lax.ppermute(lax.slice_in_dim(block, 0, width, axis=dim), axis, backward)
        block = jnp.concatenate([low, block, high], axis=dim)
    return block


def from_partner(block, axis, apart):
    count = lax.axis_size(axis)
    route = []
    for low in range(count):
        high = low | 1 << apart
        if high != low and high < count:
            route += [(low, high), (high, low)]
    return lax.ppermute(block, axis, route)


def passed_along(block, axis, distance):
    devices = range(lax.axis_size(axis))
    route = [((i - distance) % len(devices), i) for i in devices]
    return lax.ppermute(block, axis, route)


def silu_slope(values):
    sigma = jax.nn.sigmoid(values)
    return sigma * (1.0 + values * (1.0 - sigma))


def target_onehot(edge_block):
    return (edge_block[:, 1, :][:, None, :] == lax.iota(jnp.int32, 64)[None, :, None]).astype(
        jnp.bfloat16
    )


def contributions(grad_panel, edge_block, dst_onehot, rel_table, slot_base, slot_count):
    tile_count = edge_block.shape[0]
    slot_total = edge_block.shape[2]
    col_count = grad_panel.shape[1]
    per_edge = jnp.einsum(
        "tre,trc->tec",
        dst_onehot,
        grad_panel.reshape(tile_count, 64, col_count),
        preferred_element_type=jnp.float32,
    )
    rel_scales = jnp.take(rel_table, edge_block[:, 2, :], axis=0)
    edge_terms = (
        per_edge.reshape(tile_count, slot_total, col_count // DIM, DIM) * rel_scales[:, :, None, :]
    ).reshape(tile_count * slot_total, col_count)
    segment_ids = edge_block[:, 0, :].reshape(-1) - slot_base
    segment_ids = jnp.where(
        (segment_ids >= 0) & (segment_ids < slot_count), segment_ids, slot_count
    )
    summed = jax.ops.segment_sum(edge_terms, segment_ids, num_segments=slot_count + 1)
    return summed[:slot_count]


def body(
    entity_state,
    edge_tiles,
    query_head,
    query_relation,
    query_table,
    rel_vectors,
    mix_weight,
    mix_bias,
    cotangent,
):
    highest = lax.Precision.HIGHEST
    row_count = entity_state.shape[0]
    tile_count = edge_tiles.shape[0]
    slot_total = edge_tiles.shape[2]
    query_count = query_head.shape[0]
    col_count = query_count * DIM
    mirror_bit = lax.axis_size("node").bit_length() - 2
    first_row = lax.axis_index("node") * row_count
    entity_ids = first_row + lax.iota(jnp.int32, row_count)
    choose_rel = (
        query_relation[:, None] == lax.iota(jnp.int32, query_table.shape[0])[None, :]
    ).astype(jnp.float32)
    query_vec = jnp.dot(
        choose_rel, query_table, precision=highest, preferred_element_type=jnp.float32
    )
    head_match = (entity_ids[:, None] == query_head[None, :]).astype(jnp.float32)
    boundary = (
        (head_match[:, :, None] * query_vec[None, :, :])
        .reshape(row_count, col_count)
        .astype(jnp.bfloat16)
    )
    own_onehot = target_onehot(edge_tiles)

    def window(state_panel):
        sides = with_halo(state_panel, (("node", 0),), row_count)
        mirror = from_partner(state_panel, "node", mirror_bit)
        return jnp.concatenate([sides, mirror], axis=0)

    def run_layer(state_panel, layer_index):
        extended = window(state_panel)
        gathered = jnp.take(extended, edge_tiles[:, 0, :], axis=0)
        rel_scales = jnp.take(rel_vectors[layer_index], edge_tiles[:, 2, :], axis=0)
        message = (
            gathered.reshape(tile_count, slot_total, query_count, DIM) * rel_scales[:, :, None, :]
        ).astype(jnp.bfloat16)
        message = message.reshape(tile_count, slot_total, col_count)
        summed = jnp.einsum(
            "tre,tec->trc", own_onehot, message, preferred_element_type=jnp.float32
        ).reshape(row_count, col_count)
        mixed_in = boundary.astype(jnp.float32) + summed
        update = (
            jnp.einsum(
                "rqd,de->rqe",
                mixed_in.reshape(row_count, query_count, DIM),
                mix_weight[layer_index],
                precision=highest,
            )
            + mix_bias[layer_index]
        )
        result = (
            state_panel.astype(jnp.float32) + jax.nn.silu(update).reshape(row_count, col_count)
        ).astype(jnp.bfloat16)
        return (mixed_in, update, result)

    mixed_zero, update_zero, state_one = run_layer(entity_state, 0)
    mixed_one, update_one, state_two = run_layer(state_one, 1)
    grad_out = cotangent.astype(jnp.float32)
    grad_update_one = grad_out.reshape(row_count, query_count, DIM) * silu_slope(update_one)
    weight_one = jnp.einsum(
        "rqd,rqe->de",
        mixed_one.reshape(row_count, query_count, DIM),
        grad_update_one,
        precision=highest,
    )
    bias_one = jnp.sum(grad_update_one, axis=(0, 1))
    grad_mixed_one = (
        jnp.einsum("rqe,de->rqd", grad_update_one, mix_weight[1], precision=highest)
        .reshape(row_count, col_count)
        .astype(jnp.bfloat16)
    )
    window_terms = contributions(
        grad_mixed_one, edge_tiles, own_onehot, rel_vectors[1], 0, 4 * row_count
    )
    own_terms = window_terms[row_count : 2 * row_count]
    back_right = passed_along(window_terms[:row_count].astype(jnp.bfloat16), "node", -1)
    back_left = passed_along(
        window_terms[2 * row_count : 3 * row_count].astype(jnp.bfloat16), "node", 1
    )
    back_mirror = from_partner(
        window_terms[3 * row_count :].astype(jnp.bfloat16), "node", mirror_bit
    )
    adjoint_sum = (
        own_terms
        + back_right.astype(jnp.float32)
        + back_left.astype(jnp.float32)
        + back_mirror.astype(jnp.float32)
    )
    grad_state_one = grad_out + adjoint_sum
    grad_update_zero = grad_state_one.reshape(row_count, query_count, DIM) * silu_slope(update_zero)
    weight_zero = jnp.einsum(
        "rqd,rqe->de",
        mixed_zero.reshape(row_count, query_count, DIM),
        grad_update_zero,
        precision=highest,
    )
    bias_zero = jnp.sum(grad_update_zero, axis=(0, 1))
    weight_grads, bias_grads = lax.psum(
        (jnp.stack([weight_zero, weight_one]), jnp.stack([bias_zero, bias_one])), ("node", "query")
    )
    return (state_two, weight_grads, bias_grads)


def solution(mesh):
    placed = (
        P("node", "query"),
        P("node", None, None),
        P("query"),
        P("query"),
        P(),
        P(),
        P(),
        P(),
        P("node", "query"),
    )
    return jax.shard_map(
        body, mesh=mesh, in_specs=placed, out_specs=(P("node", "query"), P(), P()), check_vma=False
    )
```

profile of v0, /device:TPU:10, one launch (start us, length us, event | category | flops | bytes accessed | tf_op | source)
XLA Modules:
  0.0 605.2 jit_solution(7824408644575339123)
XLA Ops:
  11.0 27.8 %gather_fusion.1 = f32[8192,32]{1,0:T(8,128)} fusion(f32[822,32]{1,0:T(8,128)S(1)} %bitcast.102, s32[8192]{0:T(1024)S(1)} %broadcast_clamp_fusion), kind=kCustom, calls=%fused_computation.1.clone | custom fusion | bytes 2129920 | tf_op jit(solution)/shard_map/jit(_take)/gather | solution.py:114
  38.7 27.7 %gather_fusion.3 = f32[8192,32]{1,0:T(8,128)} fusion(f32[822,32]{1,0:T(8,128)S(1)} %bitcast.101, s32[8192]{0:T(1024)S(1)} %broadcast_clamp_fusion), kind=kCustom, calls=%fused_computation.3.clone | custom fusion | bytes 2129920 | tf_op jit(solution)/shard_map/jit(_take)/gather | solution.py:114
  66.5 7.5 %broadcast_select_fusion = (f32[16,512,32]{2,1,0:T(8,128)}, f32[16,512,32]{2,1,0:T(8,128)}) fusion(f32[16,512,32]{2,1,0:T(8,128)} %bitcast.109, pred[16,512]{1,0:T(8,128)(4,1)S(1)} %get-tuple-element.20, f32[16,512,32]{2,1,0:T(8,128)} %bitcast.108), kind=kLoop, calls=%fused_computation.25 | loop fusion | flops 524288 | bytes 4202496 | tf_op jit(solution)/shard_map/jit(_take)/select_n | solution.py:114
  97.1 17.7 %copy.64 = f32[64,8,16,512]{3,1,2,0:T(8,128)} copy(f32[64,8,16,512]{3,2,1,0:T(8,128)S(1)} %bitcast.105) | data formatting | bytes 33554432
  118.4 36.5 %gather_fusion = bf16[8192,512]{1,0:T(8,128)(2,1)} fusion(bf16[4096,512]{1,0:T(8,128)(2,1)} %pad_maximum_fusion, s32[8192]{0:T(1024)S(1)} %broadcast_clamp_fusion.1), kind=kCustom, calls=%fused_computation.clone | custom fusion | bytes 16809984 | tf_op jit(solution)/shard_map/jit(_take)/gather | solution.py:113
  154.9 12.4 %copy.28 = bf16[16,512,512]{1,2,0:T(8,128)(2,1)} copy(bf16[16,512,512]{2,1,0:T(8,128)(2,1)} %bitcast.107) | data formatting | bytes 16777216 | tf_op jit(solution)/shard_map/jit(_take)/gather | solution.py:113
  167.4 9.7 %fusion.1 = bf16[16,512,512]{1,2,0:T(8,128)(2,1)} fusion(bf16[16,512,512]{1,2,0:T(8,128)(2,1)} %copy.28, f32[16,512,32]{1,2,0:T(8,128)} %copy.30, pred[16,512]{1,0:T(8,128)(4,1)S(1)} %get-tuple-element.19), kind=kLoop, calls=%fused_computation.8 | loop fusion | flops 16777216 | bytes 17833984 | tf_op jit(solution)/shard_map/convert_element_type | solution.py:117
  177.0 8.0 %convert_add_fusion.3 = (f32[16,64,512]{2,1,0:T(8,128)}, f32[16,64,512]{2,1,0:T(8,128)}) fusion(f32[16,64,512]{2,1,0:T(8,128)S(1)} %copy.27, f32[512]{0:T(512)S(1)} %mul.88, bf16[16,512,512]{1,2,0:T(8,128)(2,1)} %fusion.1, s32[16,512]{1,0:T(8,128)S(1)} %get-tuple-element.18), kind=kOutput, calls=%fused_computation.16 | convolution fusion | flops 539492352 | bytes 14714880 | tf_op jit(solution)/shard_map/tre,tec->trc/dot_general | solution.py:119
  194.8 5.9 fusion.12
  208.9 39.6 %collective-permute-done.5 = bf16[1024,512]{1,0:T(8,128)(2,1)S(1)} collective-permute-done((bf16[1024,512]{1,0:T(8,128)(2,1)S(1)}, bf16[1024,512]{1,0:T(8,128)(2,1)S(1)}, u32[]{:S(2)}, u32[]{:S(2)}) %collective-permute-start.5) | collective-permute-done | bytes 1048608 | tf_op jit(solution)/shard_map/ppermute | solution.py:30
  248.4 24.0 %collective-permute-done.4 = bf16[1024,512]{1,0:T(8,128)(2,1)S(1)} collective-permute-done((bf16[1024,512]{1,0:T(8,128)(2,1)S(1)}, bf16[1024,512]{1,0:T(8,128)(2,1)S(1)}, u32[]{:S(2)}, u32[]{:S(2)}) %collective-permute-start.4) | collective-permute-done | bytes 1048608 | tf_op jit(solution)/shard_map/ppermute | solution.py:18
  274.8 36.5 %gather_fusion.2 = bf16[8192,512]{1,0:T(8,128)(2,1)} fusion(bf16[4096,512]{1,0:T(8,128)(2,1)} %pad_maximum_fusion.1, s32[8192]{0:T(1024)S(1)} %broadcast_clamp_fusion.1), kind=kCustom, calls=%fused_computation.2.clone | custom fusion | bytes 16809984 | tf_op jit(solution)/shard_map/jit(_take)/gather | solution.py:113
  311.4 12.3 %copy.35 = bf16[16,512,512]{1,2,0:T(8,128)(2,1)} copy(bf16[16,512,512]{2,1,0:T(8,128)(2,1)} %bitcast.106) | data formatting | bytes 16777216 | tf_op jit(solution)/shard_map/jit(_take)/gather | solution.py:113
  323.7 9.7 %fusion = bf16[16,512,512]{1,2,0:T(8,128)(2,1)} fusion(bf16[16,512,512]{1,2,0:T(8,128)(2,1)} %copy.35, f32[16,512,32]{1,2,0:T(8,128)} %copy.37, pred[16,512]{1,0:T(8,128)(4,1)S(1)} %get-tuple-element.19), kind=kLoop, calls=%fused_computation.6 | loop fusion | flops 16777216 | bytes 17833984 | tf_op jit(solution)/shard_map/convert_element_type | solution.py:117
  333.3 8.0 %convert_add_fusion.2 = (f32[16,64,512]{2,1,0:T(8,128)}, f32[16,64,512]{2,1,0:T(8,128)}) fusion(f32[16,64,512]{2,1,0:T(8,128)S(1)} %copy.27, f32[512]{0:T(512)S(1)} %mul.88, bf16[16,512,512]{1,2,0:T(8,128)(2,1)} %fusion, s32[16,512]{1,0:T(8,128)S(1)} %get-tuple-element.18), kind=kOutput, calls=%fused_computation.15 | convolution fusion | flops 539492352 | bytes 14714880 | tf_op jit(solution)/shard_map/tre,tec->trc/dot_general | solution.py:119
  349.7 5.8 fusion.37
  360.5 8.2 %fusion.9 = f32[16,512,512]{2,1,0:T(8,128)} fusion(bf16[16,64,512]{1,0,2:T(8,128)(2,1)S(1)} %convert_element_type.93, s32[16,512]{1,0:T(8,128)S(1)} %get-tuple-element.18), kind=kOutput, calls=%fused_computation.23 | convolution fusion | flops 537395200 | bytes 17858560 | tf_op jit(solution)/shard_map/tre,trc->tec/dot_general | solution.py:54
  368.7 17.4 %copy.47 = f32[8192,512]{0,1:T(8,128)} copy(f32[8192,512]{1,0:T(8,128)} %bitcast.104) | data formatting | bytes 33554432 | tf_op jit(solution)/shard_map/reshape | solution.py:62
  386.1 17.8 %mul.105 = f32[8192,512]{0,1:T(8,128)} multiply(f32[8192,512]{0,1:T(8,128)} %copy.47, f32[8192,512]{0,1:T(8,128)} %bitcast.103) | non-fusion elementwise | flops 4194304 | bytes 50331648 | tf_op jit(solution)/shard_map/mul | solution.py:62
  403.9 17.4 %copy.48 = f32[8192,512]{1,0:T(8,128)} copy(f32[8192,512]{0,1:T(8,128)} %mul.105) | data formatting | bytes 33554432 | tf_op jit(solution)/shard_map/mul | solution.py:62
  421.4 52.9 %scatter_custom_fusion = f32[4097,512]{1,0:T(8,128)} fusion(s32[8192]{0:T(1024)S(1)} %bitcast.117, f32[8192,512]{1,0:T(8,128)} %copy.48, f32[]{:T(128)} %constant.12.clone.1), kind=kCustom, calls=%fused_computation.9 | custom fusion | flops 4194304 | bytes 8391168 | tf_op jit(solution)/shard_map/scatter-add | solution.py:68
  508.2 21.5 %collective-permute-done.6 = bf16[1024,512]{1,0:T(8,128)(2,1)} collective-permute-done((bf16[1024,512]{1,0:T(8,128)(2,1)}, bf16[1024,512]{1,0:T(8,128)(2,1)}, u32[]{:S(2)}, u32[]{:S(2)}) %collective-permute-start.6) | collective-permute-done | bytes 1048608 | tf_op jit(solution)/shard_map/ppermute | solution.py:36
  529.7 17.9 %collective-permute-done.7 = bf16[1024,512]{1,0:T(8,128)(2,1)} collective-permute-done((bf16[1024,512]{1,0:T(8,128)(2,1)}, bf16[1024,512]{1,0:T(8,128)(2,1)}, u32[]{:S(2)}, u32[]{:S(2)}) %collective-permute-start.7) | collective-permute-done | bytes 1048608 | tf_op jit(solution)/shard_map/ppermute | solution.py:36
  560.2 44.8 %all-reduce = (f32[2,32,32]{2,1,0:T(8,128)}, f32[2,32]{1,0:T(2,128)}) all-reduce(f32[2,32,32]{2,1,0:T(8,128)S(1)} %pad_maximum_fusion.2, f32[2,32]{1,0:T(2,128)S(1)} %pad_maximum_fusion.3), channel_id=1, replica_groups=mesh['node'=8,'query'=4] {'node','query'}, use_global_device_ids=true, to_apply=%region_1.0 | all-reduce | flops 2112 | bytes 16896 | tf_op jit(solution)/shard_map/psum | solution.py:179
  (102 shorter events, 117.0 us)
Async XLA Ops:
  0.6 73.3 %copy-start = (f32[822,32]{0,1:T(8,128)S(1)}, f32[822,32]{0,1:T(8,128)}, u32[]{:S(2)}) copy-start(f32[822,32]{0,1:T(8,128)} %param.17) | copy-start | bytes 315652
  0.6 114.2 %collective-permute-start.1 = (bf16[1024,512]{1,0:T(8,128)(2,1)}, bf16[1024,512]{1,0:T(8,128)(2,1)}, u32[]{:S(2)}, u32[]{:S(2)}) collective-permute-start(bf16[1024,512]{1,0:T(8,128)(2,1)} %param.13), channel_id=1, source_target_pairs={{4,0},{8,4},{12,8},{16,12},{20,16},{24,20},{28,24},{0,28},{5,1},{9... | collective-permute-start | bytes 3145736 | tf_op jit(solution)/shard_map/ppermute | solution.py:18
  1.2 113.6 %collective-permute-start = (bf16[1024,512]{1,0:T(8,128)(2,1)}, bf16[1024,512]{1,0:T(8,128)(2,1)}, u32[]{:S(2)}, u32[]{:S(2)}) collective-permute-start(bf16[1024,512]{1,0:T(8,128)(2,1)} %param.13), channel_id=1, source_target_pairs={{0,4},{4,8},{8,12},{12,16},{16,20},{20,24},{24,28},{28,0},{1,5},{5... | collective-permute-start | bytes 3145736 | tf_op jit(solution)/shard_map/ppermute | solution.py:15
  3.6 111.2 %collective-permute-start.2 = (bf16[1024,512]{1,0:T(8,128)(2,1)}, bf16[1024,512]{1,0:T(8,128)(2,1)}, u32[]{:S(2)}, u32[]{:S(2)}) collective-permute-start(bf16[1024,512]{1,0:T(8,128)(2,1)} %param.13), channel_id=1, source_target_pairs={{0,16},{16,0},{4,20},{20,4},{8,24},{24,8},{12,28},{28,12},{1,17},{... | collective-permute-start | bytes 3145736 | tf_op jit(solution)/shard_map/ppermute | solution.py:30
  66.5 7.5 %copy-start.17 = (s32[16]{0:T(128)S(1)}, s32[16]{0:T(128)}, u32[]{:S(2)}) copy-start(s32[16]{0:T(128)} %param.16) | copy-start | bytes 196
  74.2 7.4 %copy-start.13 = (f32[16,32]{1,0:T(8,128)}, f32[16,32]{1,0:T(8,128)S(1)}, u32[]{:S(2)}) copy-start(f32[16,32]{1,0:T(8,128)S(1)} %fusion.24) | copy-start | bytes 6148
  78.0 3.7 copy-start.12
  78.0 3.8 copy-start.18
  97.1 17.8 %copy-start.16 = (f32[2,32]{1,0:T(2,128)S(1)}, f32[2,32]{1,0:T(2,128)}, u32[]{:S(2)}) copy-start(f32[2,32]{1,0:T(2,128)} %param.20) | copy-start | bytes 772
  97.1 17.8 %copy-start.9 = (bf16[1024,512]{1,0:T(8,128)(2,1)S(1)}, bf16[1024,512]{1,0:T(8,128)(2,1)}, u32[]{:S(2)}) copy-start(bf16[1024,512]{1,0:T(8,128)(2,1)} %param.13) | copy-start | bytes 3145732
  189.9 4.9 copy-start.15
  205.7 66.7 %copy-start.2 = (bf16[1024,512]{1,0:T(8,128)(2,1)}, bf16[1024,512]{1,0:T(8,128)(2,1)S(1)}, u32[]{:S(2)}) copy-start(bf16[1024,512]{1,0:T(8,128)(2,1)S(1)} %add_convert_fusion.1) | copy-start | bytes 3145732
  205.8 42.7 %collective-permute-start.5 = (bf16[1024,512]{1,0:T(8,128)(2,1)S(1)}, bf16[1024,512]{1,0:T(8,128)(2,1)S(1)}, u32[]{:S(2)}, u32[]{:S(2)}) collective-permute-start(bf16[1024,512]{1,0:T(8,128)(2,1)S(1)} %add_convert_fusion.1), channel_id=1, source_target_pairs={{0,16},{16,0},{4,20},{20,4},{8,24},{24,8},{12,28},{28,12},{1,17},{... | collective-permute-start | bytes 3145736 | tf_op jit(solution)/shard_map/ppermute | solution.py:30
  205.8 66.6 %collective-permute-start.4 = (bf16[1024,512]{1,0:T(8,128)(2,1)S(1)}, bf16[1024,512]{1,0:T(8,128)(2,1)S(1)}, u32[]{:S(2)}, u32[]{:S(2)}) collective-permute-start(bf16[1024,512]{1,0:T(8,128)(2,1)S(1)} %add_convert_fusion.1), channel_id=1, source_target_pairs={{4,0},{8,4},{12,8},{16,12},{20,16},{24,20},{28,24},{0,28},{5,1},{9... | collective-permute-start | bytes 3145736 | tf_op jit(solution)/shard_map/ppermute | solution.py:18
  205.9 66.6 %collective-permute-start.3 = (bf16[1024,512]{1,0:T(8,128)(2,1)S(1)}, bf16[1024,512]{1,0:T(8,128)(2,1)S(1)}, u32[]{:S(2)}, u32[]{:S(2)}) collective-permute-start(bf16[1024,512]{1,0:T(8,128)(2,1)S(1)} %add_convert_fusion.1), channel_id=1, source_target_pairs={{0,4},{4,8},{8,12},{12,16},{16,20},{20,24},{24,28},{28,0},{1,5},{5... | collective-permute-start | bytes 3145736 | tf_op jit(solution)/shard_map/ppermute | solution.py:15
  478.2 4.8 copy-start.5
  480.0 49.7 %collective-permute-start.6 = (bf16[1024,512]{1,0:T(8,128)(2,1)}, bf16[1024,512]{1,0:T(8,128)(2,1)}, u32[]{:S(2)}, u32[]{:S(2)}) collective-permute-start(bf16[1024,512]{1,0:T(8,128)(2,1)} %get-tuple-element.11), channel_id=1, source_target_pairs={{4,0},{8,4},{12,8},{16,12},{20,16},{24,20},{28,24},{0,28},{5,1},{9... | collective-permute-start | bytes 3145736 | tf_op jit(solution)/shard_map/ppermute | solution.py:36
  480.0 49.7 %collective-permute-start.8 = (bf16[1024,512]{1,0:T(8,128)(2,1)}, bf16[1024,512]{1,0:T(8,128)(2,1)}, u32[]{:S(2)}, u32[]{:S(2)}) collective-permute-start(bf16[1024,512]{1,0:T(8,128)(2,1)} %get-tuple-element.12), channel_id=1, source_target_pairs={{0,16},{16,0},{4,20},{20,4},{8,24},{24,8},{12,28},{28,12},{1,17},{... | collective-permute-start | bytes 3145736 | tf_op jit(solution)/shard_map/ppermute | solution.py:30
  481.5 66.1 %collective-permute-start.7 = (bf16[1024,512]{1,0:T(8,128)(2,1)}, bf16[1024,512]{1,0:T(8,128)(2,1)}, u32[]{:S(2)}, u32[]{:S(2)}) collective-permute-start(bf16[1024,512]{1,0:T(8,128)(2,1)} %get-tuple-element.13), channel_id=1, source_target_pairs={{28,0},{0,4},{4,8},{8,12},{12,16},{16,20},{20,24},{24,28},{29,1},{... | collective-permute-start | bytes 3145736 | tf_op jit(solution)/shard_map/ppermute | solution.py:36
  498.1 5.0 copy-start.3
  498.1 8.0 %copy-start.11 = (f32[1024,16]{0,1:T(8,128)S(1)}, f32[1024,16]{0,1:T(8,128)}, u32[]{:S(2)}) copy-start(f32[1024,16]{0,1:T(8,128)} %copy-done.10) | copy-start | bytes 196612
  498.1 8.0 %copy-start.14 = (f32[16,32]{1,0:T(8,128)S(1)}, f32[16,32]{1,0:T(8,128)}, u32[]{:S(2)}) copy-start(f32[16,32]{1,0:T(8,128)} %copy-done.13) | copy-start | bytes 6148
  506.2 41.4 %copy-start.8 = (bf16[1024,512]{1,0:T(8,128)(2,1)S(1)}, bf16[1024,512]{1,0:T(8,128)(2,1)}, u32[]{:S(2)}) copy-start(bf16[1024,512]{1,0:T(8,128)(2,1)} %param.21) | copy-start | bytes 3145732
  558.2 46.8 %copy-start.1 = (f32[822,32]{0,1:T(8,128)S(1)}, f32[822,32]{0,1:T(8,128)}, u32[]{:S(2)}) copy-start(f32[822,32]{0,1:T(8,128)} %param.17) | copy-start | bytes 315652
  (4 other events, 10.4 us)
where the time goes:
time: 615 us; the launch traced here: 605 us
  local copies, waits for them, and re-layouts  279 us (45%)
  other arithmetic  122 us (20%)
  waiting for transfers between devices  103 us (17%)
  blocking collectives  44.8 us (7%)
  matrix products  42 us (7%)
  starting transfers between devices  13.3 us (2%)
    gather x4, local copies, waits for them, and re-layouts, run_layer(): gathered = jnp.take(extended, edge_tiles[:, 0, :], axis=0)  97.8 us
    gather x2, local copies, waits for them, and re-layouts, run_layer(): rel_scales = jnp.take(rel_vectors[layer_index], edge_tiles[:, 2, :], axis=0)  55.5 us
    scatter-add x1, other arithmetic, contributions(): jax.ops.segment_sum(edge_terms, segment_ids, num_segments=slot_count + 1)  52.9 us
    psum x1, blocking collectives, body(): lax.psum((jnp.stack([weight_zero, weight_one]), jnp.stack([bias_zero, bia...  44.8 us
    ppermute x3, waiting for transfers between devices, from_partner(): return lax.ppermute(block, axis, route)  39.6 us
    ppermute x2, waiting for transfers between devices, passed_along(): return lax.ppermute(block, axis, route)  39.4 us
    ppermute x2, waiting for transfers between devices, with_halo(): lax.ppermute(lax.slice_in_dim(block, 0, width, axis=dim), axis, backward)  24 us
    unnamed x46, local copies, waits for them, and re-layouts  23.4 us
  transfers between devices with their start and end apart: 9, of which 4 were waited for; matrix products, arithmetic and copies ran while one was open for 22% of the time, Pallas kernels for 0%

commit v1 on v0

v1 whole, which is shorter than its diff:
```python
import functools

import jax
import jax.numpy as jnp
from jax import lax
from jax.experimental import pallas as pl
from jax.experimental.pallas import tpu as pltpu
from jax.sharding import PartitionSpec as P

DIM = 32
LANES = 128
UNROLL = 24
SUMS = 3
CHUNK = 256
AXES = ("node", "query")
HIGHEST = lax.Precision.HIGHEST
SMEM = pl.BlockSpec(memory_space=pltpu.SMEM)
VMEM = pl.BlockSpec(memory_space=pltpu.VMEM)


def silu_slope(values):
    sigma = jax.nn.sigmoid(values)
    return sigma * (1.0 + values * (1.0 - sigma))


class Seats:
    def __init__(self, nodes, queries):
        self.nodes, self.queries = nodes, queries

    def home(self, part, column):
        return part * self.queries + column

    def seat(self, part, column):
        half = self.nodes // 2
        low = part % half
        node = (column & 1) * half + (low ^ (low >> 1))
        return node * self.queries + (column >> 1) * 2 + part // half

    def blocks(self):
        return [(p, c) for p in range(self.nodes) for c in range(self.queries)]

    def gather(self):
        return [(self.home(p, c), self.seat(p, c)) for p, c in self.blocks()]

    def give_back(self):
        return [(target, source) for source, target in self.gather()]

    def shift(self, step):
        return [
            (self.seat((p - step) % self.nodes, c), self.seat(p, c)) for p, c in self.blocks()
        ]

    def mirror(self):
        return [
            (self.seat(p, c), self.seat((p + self.nodes // 2) % self.nodes, c))
            for p, c in self.blocks()
        ]

    def parts(self):
        table = [0] * (self.nodes * self.queries)
        for p, c in self.blocks():
            table[self.seat(p, c)] = p
        return table


def spread(block_ref, window_ref, first):
    if block_ref.shape[1] == LANES:
        rows = block_ref.shape[0]

        def step(i, carry):
            at = pl.multiple_of(i * CHUNK, CHUNK)
            window_ref[pl.ds(first + at, CHUNK), :] = block_ref[pl.ds(at, CHUNK), :].astype(
                jnp.float32
            )
            return carry

        lax.fori_loop(0, rows // CHUNK, step, 0)
        return
    rows, cols = block_ref.shape
    groups = cols // LANES
    size = CHUNK // groups

    def step(i, carry):
        at = pl.multiple_of(i * size, size)
        for j in range(groups):
            window_ref[pl.ds(first + at * groups + j, size, stride=groups), :] = block_ref[
                pl.ds(at, size), j * LANES : (j + 1) * LANES
            ].astype(jnp.float32)
        return carry

    lax.fori_loop(0, rows // size, step, 0)


def clear(sums):
    def step(i, carry):
        at = pl.multiple_of(i * CHUNK, CHUNK)
        for ref in sums:
            ref[pl.ds(at, CHUNK), :] = jnp.zeros((CHUNK, LANES), jnp.float32)
        return carry

    lax.fori_loop(0, sums[0].shape[0] // CHUNK, step, 0)


def walk(groups, begin, end, from_ref, to_ref, rel_ref, window, table, sums):
    def step(i, carry):
        first = begin + i * UNROLL
        for u in range(UNROLL):
            source = pl.multiple_of(from_ref[first + u], groups)
            target = pl.multiple_of(to_ref[first + u], groups)
            scale = table[pl.ds(rel_ref[first + u], groups, stride=0), :]
            sums[u % SUMS][pl.ds(target, groups), :] += (
                window[pl.ds(source, groups), :] * scale
            )
        return carry

    lax.fori_loop(0, (end - begin) // UNROLL, step, 0)


def total_of(sums, at):
    value = sums[0][pl.ds(at, CHUNK), :]
    for ref in sums[1:]:
        value = value + ref[pl.ds(at, CHUNK), :]
    return value


def bucket_kernel(pos_ref, word_ref, count_ref, out_ref, *, edges, dummy):
    unroll = 16

    def step(i, carry):
        for u in range(unroll):
            out_ref[pos_ref[i * unroll + u]] = word_ref[i * unroll + u]
        return carry

    lax.fori_loop(0, edges // unroll, step, 0)

    def fill(i, carry):
        out_ref[i] = dummy
        return carry

    for k in range(4):
        lax.fori_loop(count_ref[k], count_ref[k + 4], fill, 0)


def near_kernel(groups, ends, source, target, rel, own, mirror, table, out, window, *sums):
    half = window.shape[0] // 2
    spread(own, window, 0)
    spread(mirror, window, half)
    clear(sums)
    walk(groups, 0, ends[1], source, target, rel, window, table, sums)

    def step(i, carry):
        at = pl.multiple_of(i * CHUNK, CHUNK)
        out[pl.ds(at, CHUNK), :] = total_of(sums, at)
        return carry

    lax.fori_loop(0, half // CHUNK, step, 0)


def add_boundary(groups, heads, head_rows, ref):
    for q in range(head_rows.shape[0]):
        row = heads[q]

        @pl.when((row >= 0) & (row < ref.shape[0] // groups))
        def _():
            at = row * groups + q * DIM // LANES
            ref[pl.ds(at, 1), :] += head_rows[q : q + 1, :]


def far_sums(groups, ends, source, target, rel, left, right, near, table, heads, head_rows, window, sums):
    half = window.shape[0] // 2
    spread(left, window, 0)
    spread(right, window, half)
    clear(sums[1:])

    def step(i, carry):
        at = pl.multiple_of(i * CHUNK, CHUNK)
        sums[0][pl.ds(at, CHUNK), :] = near[pl.ds(at, CHUNK), :]
        return carry

    lax.fori_loop(0, half // CHUNK, step, 0)
    add_boundary(groups, heads, head_rows, sums[0])
    walk(groups, ends[1], ends[3], source, target, rel, window, table, sums)


def times(left, right):
    return jnp.dot(left, right, precision=HIGHEST, preferred_element_type=jnp.float32)


def outer(left, right):
    return lax.dot_general(
        left, right, (((0,), (0,)), ((), ())), precision=HIGHEST, preferred_element_type=jnp.float32
    )


def first_kernel(
    groups, ends, heads, source, target, rel, left, right, near, own, table, head_rows, weight, bias,
    state, mixed, update, window, *sums,
):
    far_sums(groups, ends, source, target, rel, left, right, near, table, heads, head_rows, window, sums)
    spread(own, window, 0)

    def step(i, carry):
        at = pl.multiple_of(i * CHUNK, CHUNK)
        mix = total_of(sums, at)
        values = times(mix, weight[...]) + bias[...]
        mixed[pl.ds(at, CHUNK), :] = mix
        update[pl.ds(at, CHUNK), :] = values
        state[pl.ds(at, CHUNK), :] = (
            window[pl.ds(at, CHUNK), :] + values * jax.nn.sigmoid(values)
        ).astype(jnp.bfloat16)
        return carry

    lax.fori_loop(0, mixed.shape[0] // CHUNK, step, 0)


def second_kernel(
    groups, ends, heads, source, target, rel, left, right, near, own, table, head_rows, weight, bias,
    weight_back, cotangent, state, grad_mixed, weight_sum, bias_sum, window, *sums,
):
    far_sums(groups, ends, source, target, rel, left, right, near, table, heads, head_rows, window, sums)
    half = window.shape[0] // 2
    spread(own, window, 0)
    spread(cotangent, window, half)
    weight_sum[...] = jnp.zeros_like(weight_sum)
    bias_sum[...] = jnp.zeros_like(bias_sum)

    def step(i, carry):
        at = pl.multiple_of(i * CHUNK, CHUNK)
        mix = total_of(sums, at)
        values = times(mix, weight[...]) + bias[...]
        window[pl.ds(at, CHUNK), :] += values * jax.nn.sigmoid(values)
        grad = window[pl.ds(half + at, CHUNK), :] * silu_slope(values)
        grad_mixed[pl.ds(at, CHUNK), :] = times(grad, weight_back[...]).astype(jnp.bfloat16)
        weight_sum[...] += outer(mix, grad)
        bias_sum[...] += jnp.sum(grad, axis=0, keepdims=True)
        return carry

    lax.fori_loop(0, half // CHUNK, step, 0)
    rows = state.shape[0]
    size = CHUNK // groups

    def store(i, carry):
        at = pl.multiple_of(i * size, size)
        for j in range(groups):
            state[pl.ds(at, size), j * LANES : (j + 1) * LANES] = window[
                pl.ds(at * groups + j, size, stride=groups), :
            ].astype(jnp.bfloat16)
        return carry

    lax.fori_loop(0, rows // size, store, 0)


def adjoint_kernel(groups, kinds, ends, source, target, rel, grad_mixed, table, *refs):
    outs, window, sums = refs[: len(kinds)], refs[len(kinds)], refs[len(kinds) + 1 :]
    spread(grad_mixed, window, 0)
    for kind, out in zip(kinds, outs):
        clear(sums)
        begin = ends[kind - 1] if kind else 0
        walk(groups, begin, ends[kind], target, source, rel, window, table, sums)

        def step(i, carry):
            at = pl.multiple_of(i * CHUNK, CHUNK)
            out[pl.ds(at, CHUNK), :] = total_of(sums, at).astype(out.dtype)
            return carry

        lax.fori_loop(0, window.shape[0] // CHUNK, step, 0)


def folded(wide):
    value = wide[:DIM, :DIM]
    for g in range(1, LANES // DIM):
        value = value + wide[g * DIM : (g + 1) * DIM, g * DIM : (g + 1) * DIM]
    return value


def folded_row(wide):
    value = wide[:, :DIM]
    for g in range(1, LANES // DIM):
        value = value + wide[:, g * DIM : (g + 1) * DIM]
    return value


def last_kernel(
    groups, cotangent, own, left, right, mirror, update, mixed, weight_one, bias_one, out, window,
    weight_sum, bias_sum,
):
    spread(cotangent, window, 0)
    weight_sum[...] = jnp.zeros_like(weight_sum)
    bias_sum[...] = jnp.zeros_like(bias_sum)

    def step(i, carry):
        rows = pl.ds(pl.multiple_of(i * CHUNK, CHUNK), CHUNK)
        state_grad = window[rows, :] + own[rows, :]
        for ref in (left, right, mirror):
            state_grad = state_grad + ref[rows, :].astype(jnp.float32)
        grad = state_grad * silu_slope(update[rows, :])
        weight_sum[...] += outer(mixed[rows, :], grad)
        bias_sum[...] += jnp.sum(grad, axis=0, keepdims=True)
        return carry

    lax.fori_loop(0, window.shape[0] // CHUNK, step, 0)
    out[...] = jnp.zeros_like(out)
    out[0:DIM, 0:DIM] = folded(weight_sum[...])
    out[DIM : 2 * DIM, 0:DIM] = folded(weight_one[...])
    out[2 * DIM : 2 * DIM + 1, 0:DIM] = folded_row(bias_sum[...])
    out[2 * DIM + 1 : 2 * DIM + 2, 0:DIM] = folded_row(bias_one[...])


def edge_lists(edges, row_count, groups, rel_count):
    tile_count, slot_total = edges.shape[0], edges.shape[2]
    edge_count = tile_count * slot_total
    lines = edge_count // LANES
    slots = edges[:, 0, :].reshape(lines, LANES)
    rows = (edges[:, 1, :] + 64 * lax.iota(jnp.int32, tile_count)[:, None]).reshape(lines, LANES)
    rels = edges[:, 2, :].reshape(lines, LANES)
    quarter = slots // row_count
    local = slots % row_count
    kind = jnp.where(
        quarter == 1, 0, jnp.where(quarter == 3, 1, jnp.where(quarter == 0, 2, 3))
    )
    row_bits = (row_count - 1).bit_length()
    word = (rels << (2 * row_bits + 1)) | (rows << (row_bits + 1)) | ((kind & 1) * row_count + local)
    onehot = (kind[None] == lax.iota(jnp.int32, 4)[:, None, None]).astype(jnp.bfloat16)
    upto = (lax.iota(jnp.int32, LANES)[:, None] <= lax.iota(jnp.int32, LANES)[None, :]).astype(
        jnp.bfloat16
    )
    within = jnp.einsum("krl,lm->krm", onehot, upto, preferred_element_type=jnp.float32)
    per_line = within[:, :, -1]
    above = (lax.iota(jnp.int32, lines)[:, None] > lax.iota(jnp.int32, lines)[None, :]).astype(
        jnp.bfloat16
    )
    before = jnp.einsum(
        "rs,ks->kr", above, per_line.astype(jnp.bfloat16), preferred_element_type=jnp.float32
    )
    counts = jnp.sum(per_line, axis=1).astype(jnp.int32)
    padded = (counts + UNROLL - 1) // UNROLL * UNROLL
    ends = jnp.sum(
        jnp.where(lax.iota(jnp.int32, 4)[:, None] >= lax.iota(jnp.int32, 4)[None, :], padded[None], 0),
        axis=1,
    )
    begins = ends - padded
    place = begins.astype(jnp.float32)[:, None, None] + before[:, :, None] + within - 1.0
    pos = jnp.sum(jnp.where(onehot > 0, place, 0.0), axis=0).astype(jnp.int32)
    room = (edge_count + 4 * UNROLL + LANES - 1) // LANES * LANES
    words = pl.pallas_call(
        functools.partial(
            bucket_kernel, edges=edge_count, dummy=rel_count << (2 * row_bits + 1)
        ),
        out_shape=jax.ShapeDtypeStruct((room,), jnp.int32),
        in_specs=[SMEM] * 3,
        out_specs=SMEM,
        name="bucket",
    )(pos.reshape(-1), word.reshape(-1), jnp.concatenate([begins + counts, ends]))
    source = (words & (2 * row_count - 1)) * groups
    target = ((words >> (row_bits + 1)) & (row_count - 1)) * groups
    return ends, source, target, words >> (2 * row_bits + 1)


def body(
    entity_state,
    edge_tiles,
    query_head,
    query_relation,
    query_table,
    rel_vectors,
    mix_weight,
    mix_bias,
    cotangent,
):
    row_count, col_count = entity_state.shape
    groups = col_count // LANES
    long = row_count * groups
    query_count = query_head.shape[0]
    rel_count = rel_vectors.shape[1]
    seats = Seats(lax.axis_size("node"), lax.axis_size("query"))

    def send(block, route):
        return lax.ppermute(block, AXES, route)

    def kernel(fn, outs, specs, scratch, name):
        return pl.pallas_call(
            fn, out_shape=outs, in_specs=specs, out_specs=[VMEM] * len(outs), scratch_shapes=scratch,
            name=name,
        )

    wide_f32 = jax.ShapeDtypeStruct((long, LANES), jnp.float32)
    wide_bf16 = jax.ShapeDtypeStruct((long, LANES), jnp.bfloat16)
    pair = pltpu.VMEM((2 * long, LANES), jnp.float32)
    single = pltpu.VMEM((long, LANES), jnp.float32)
    sums = [single] * SUMS

    state_zero = send(entity_state, seats.gather())
    flat = jnp.concatenate([edge_tiles.reshape(-1), query_head, query_relation])
    edge_total = edge_tiles.size
    flat = jnp.pad(flat, (0, -flat.shape[0] % (8 * LANES))).reshape(-1, LANES)
    flat = send(flat, seats.gather()).reshape(-1)
    edges = flat[:edge_total].reshape(edge_tiles.shape)
    own_head = flat[edge_total : edge_total + query_count]
    own_relation = flat[edge_total + query_count : edge_total + 2 * query_count]
    moved = lax.optimization_barrier((cotangent, state_zero))
    grad_out = send(moved[0], seats.gather())
    state_zero = moved[1]

    linear = lax.axis_index("node") * seats.queries + lax.axis_index("query")
    part = jnp.array(seats.parts(), jnp.int32)[linear]
    heads = own_head - part * row_count
    choose_rel = (own_relation[:, None] == lax.iota(jnp.int32, query_table.shape[0])[None, :]).astype(
        jnp.float32
    )
    query_vec = (
        jnp.dot(choose_rel, query_table, precision=HIGHEST, preferred_element_type=jnp.float32)
        .astype(jnp.bfloat16)
        .astype(jnp.float32)
    )
    repeat = LANES // DIM
    lane_group = lax.iota(jnp.int32, LANES) // DIM
    head_rows = jnp.where(
        lane_group[None, :] == (lax.iota(jnp.int32, query_count) % repeat)[:, None],
        jnp.tile(query_vec, (1, repeat)),
        0.0,
    )
    tables = jnp.tile(jnp.pad(rel_vectors, ((0, 0), (0, -rel_count % 8 or 8), (0, 0))), (1, 1, repeat))
    same = lane_group[:, None] == lane_group[None, :]
    weights = jnp.where(same[None], jnp.tile(mix_weight, (1, repeat, repeat)), 0.0)
    weight_back = weights[1].T
    biases = jnp.tile(mix_bias, (1, repeat))[:, None, :]
    ends, source, target, rel = edge_lists(edges, row_count, groups, rel_count)
    source_local = source % long

    def layer(state, index, far, outs):
        mirror = send(state, seats.mirror())
        left = send(state, seats.shift(1))
        right = send(state, seats.shift(-1))
        (near,) = kernel(
            functools.partial(near_kernel, groups), [wide_f32], [SMEM] * 4 + [VMEM] * 3, [pair] + sums,
            f"near_{index}",
        )(ends, source, target, rel, state, mirror, tables[index])
        args = [left, right, near, state, tables[index], head_rows, weights[index], biases[index]]
        if index:
            args += [weight_back, grad_out]
        return kernel(
            functools.partial(far, groups), outs, [SMEM] * 5 + [VMEM] * len(args), [pair] + sums,
            f"far_{index}",
        )(ends, heads, source, target, rel, *args)

    state_one, mixed_zero, update_zero = layer(
        state_zero, 0, first_kernel, [wide_bf16, wide_f32, wide_f32]
    )
    square = jax.ShapeDtypeStruct((LANES, LANES), jnp.float32)
    line = jax.ShapeDtypeStruct((1, LANES), jnp.float32)
    state_two, grad_mixed, weight_one, bias_one = layer(
        state_one,
        1,
        second_kernel,
        [jax.ShapeDtypeStruct(entity_state.shape, jnp.bfloat16), wide_bf16, square, line],
    )

    def adjoint(kinds, outs, name):
        return kernel(
            functools.partial(adjoint_kernel, groups, kinds), outs, [SMEM] * 4 + [VMEM] * 2,
            [single] + sums, name,
        )(ends, source_local, target, rel, grad_mixed, tables[1])

    (to_left,) = adjoint((2,), [wide_bf16], "adjoint_left")
    from_right = send(to_left, seats.shift(-1))
    (to_right,) = adjoint((3,), [wide_bf16], "adjoint_right")
    from_left = send(to_right, seats.shift(1))
    own_terms, to_mirror = adjoint((0, 1), [wide_f32, wide_bf16], "adjoint_near")
    from_mirror = send(to_mirror, seats.mirror())
    final_state = send(state_two, seats.give_back())
    (grads,) = kernel(
        functools.partial(last_kernel, groups),
        [jax.ShapeDtypeStruct((2 * DIM + 8, LANES), jnp.float32)],
        [VMEM] * 9,
        [single, pltpu.VMEM((LANES, LANES), jnp.float32), pltpu.VMEM((1, LANES), jnp.float32)],
        "last",
    )(
        grad_out, own_terms, from_left, from_right, from_mirror, update_zero, mixed_zero, weight_one,
        bias_one,
    )
    devices = seats.nodes * seats.queries
    reach = 1
    while reach < devices:
        grads = grads + send(grads, [(i, i ^ reach) for i in range(devices)])
        reach *= 2
    weight_grads = grads[: 2 * DIM, :DIM].reshape(2, DIM, DIM)
    bias_grads = grads[2 * DIM : 2 * DIM + 2, :DIM]
    return (final_state, weight_grads, bias_grads)


def solution(mesh):
    placed = (
        P("node", "query"),
        P("node", None, None),
        P("query"),
        P("query"),
        P(),
        P(),
        P(),
        P(),
        P("node", "query"),
    )
    return jax.shard_map(
        body, mesh=mesh, in_specs=placed, out_specs=(P("node", "query"), P(), P()), check_vma=False
    )
```

time: 615 us -> 269 us (0.44); the launches traced: 605 us -> 266 us
  local copies, waits for them, and re-layouts: 279 us -> 19.3 us
  Pallas kernels: 0 us -> 133 us
  other arithmetic: 122 us -> 9.79 us
  blocking collectives: 44.8 us -> 0 us
  matrix products: 42 us -> 0.46 us
  waiting for transfers between devices: 103 us -> 74.7 us
  starting transfers between devices: 13.3 us -> 26.8 us
    gather x6 -> x0, local copies, waits for them, and re-layouts: 153 us -> none  [the longest x4 97.8 us: run_layer(): gathered = jnp.take(extended, edge_tiles[:, 0, :], axis=0)]
    pallas_call x0 -> x9, Pallas kernels: none -> 133 us  [the longest x2 46.5 us: layer(): kernel(functools.partial(far, groups), outs, [SMEM] * 5 + [VMEM] * len(ar...]
    scatter-add x1 -> x0, other arithmetic: 52.9 us -> none  [contributions(): jax.ops.segment_sum(edge_terms, segment_ids, num_segments=slot_count + 1)]
    psum x1 -> x0, blocking collectives: 44.8 us -> none  [body(): lax.psum((jnp.stack([weight_zero, weight_one]), jnp.stack([bias_zero, bia...]
    dot_general x9 -> x3, matrix products: 42 us -> 0.46 us  [the longest x1 0.22 us: body(): jnp.dot(choose_rel, query_table, precision=HIGHEST, preferred_element_typ...]
    reshape x5 -> x3, local copies, waits for them, and re-layouts: 31.7 us -> 0.1 us  [the longest x1 0.05 us: body(): flat = jnp.concatenate([edge_tiles.reshape(-1), query_head, query_relation])]
    ppermute x9 -> x18, waiting for transfers between devices: 103 us -> 74.7 us  [send(): return lax.ppermute(block, AXES, route)]
    mul x6 -> x0, local copies, waits for them, and re-layouts: 26.6 us -> none  [the longest x1 17.4 us: contributions(): per_edge.reshape(tile_count, slot_total, col_count // DIM, DIM)]
  transfers between devices with their start and end apart: 9 -> 18, of which waited for: 4 -> 10; matrix products, arithmetic and copies ran while one was open for 22% -> 8% of each run, Pallas kernels for 0% -> 21%
where the time goes in v1:
time: 269 us; the launch traced here: 266 us
  Pallas kernels  133 us (49%)
  waiting for transfers between devices  74.7 us (28%)
  starting transfers between devices  26.8 us (10%)
  local copies, waits for them, and re-layouts  19.3 us (7%)
  other arithmetic  9.79 us (4%)
    ppermute x18, waiting for transfers between devices, send(): return lax.ppermute(block, AXES, route)  74.7 us
    pallas_call x2, Pallas kernels, layer(): kernel(functools.partial(far, groups), outs, [SMEM] * 5 + [VMEM] * len(ar...  46.5 us
    pallas_call x3, Pallas kernels, adjoint(): kernel(functools.partial(adjoint_kernel, groups, kinds), outs, [SMEM] * 4...  31.8 us
    pallas_call x2, Pallas kernels, layer(): kernel(functools.partial(near_kernel, groups), [wide_f32], [SMEM] * 4 + [...  27.2 us
    ppermute x18, starting transfers between devices, send(): return lax.ppermute(block, AXES, route)  26.8 us
    pallas_call x1, Pallas kernels, edge_lists(): pl.pallas_call(functools.partial(bucket_kernel, edges=edge_count, dummy=r...  17.2 us
    pallas_call x1, Pallas kernels, body(): kernel(functools.partial(last_kernel, groups), [jax.ShapeDtypeStruct((2 *...  10.6 us
    unnamed x27, local copies, waits for them, and re-layouts  7.72 us
  transfers between devices with their start and end apart: 18, of which 10 were waited for; matrix products, arithmetic and copies ran while one was open for 8% of the time, Pallas kernels for 21%

profile of v1, /device:TPU:10, one launch (start us, length us, event | category | flops | bytes accessed | tf_op | source)
XLA Modules:
  0.0 265.9 jit_solution(16926472120763985401)
XLA Ops:
  2.5 2.4 collective-permute-start
  4.9 3.4 %collective-permute-start.1 = (bf16[1024,512]{1,0:T(8,128)(2,1)}, bf16[1024,512]{1,0:T(8,128)(2,1)S(1)}, u32[]{:S(2)}, u32[]{:S(2)}) collective-permute-start(bf16[1024,512]{1,0:T(8,128)(2,1)} %param.10), channel_id=1, source_target_pairs={{0,0},{1,16},{2,2},{3,18},{4,4},{5,20},{6,6},{7,22},{8,12},{9,28},... | collective-permute-start | bytes 3145736 | tf_op jit(solution)/shard_map/ppermute | solution.py:378
  20.5 12.6 %collective-permute-done.1.own = bf16[1024,512]{1,0:T(8,128)(2,1)S(1)} collective-permute-done((bf16[1024,512]{1,0:T(8,128)(2,1)}, bf16[1024,512]{1,0:T(8,128)(2,1)S(1)}, u32[]{:S(2)}, u32[]{:S(2)}) %collective-permute-start.1) | collective-permute-done | bytes 1048608 | tf_op jit(solution)/shard_map/ppermute | solution.py:378
  33.1 2.9 %collective-permute-start.3 = (bf16[1024,512]{1,0:T(8,128)(2,1)S(1)}, bf16[1024,512]{1,0:T(8,128)(2,1)S(1)}, u32[]{:S(2)}, u32[]{:S(2)}) collective-permute-start(bf16[1024,512]{1,0:T(8,128)(2,1)S(1)} %collective-permute-done.1.own), channel_id=1, source_target_pairs={{4,0},{20,16},{6,2},{22,18},{12,4},{28,20},{14,6},{30,22},{8,12},{... | collective-permute-start | bytes 3145736 | tf_op jit(solution)/shard_map/ppermute | solution.py:378
  39.5 17.2 %bucket.1 = s32[8320]{0:T(1024)} custom-call(s32[8192]{0:T(1024)} %convert_bitcast_fusion.pos_ref, s32[8192]{0:T(1024)} %fusion.12.word_ref, s32[8]{0:T(128)} %pad_add_fusion.count_ref), custom_call_target="tpu_custom_call" | custom-call | tf_op jit(solution)/shard_map/bucket/pallas_call | solution.py:345
  59.4 13.6 %near_0.1.near = f32[4096,128]{1,0:T(8,128)} custom-call(s32[4]{0:T(128)} %copy-done.9, s32[8320]{0:T(1024)} %get-tuple-element.38.source, s32[8320]{0:T(1024)} %get-tuple-element.37.target, s32[8320]{0:T(1024)} %get-tuple-element.36.rel, bf16[1024,512]{1,0:T(8,128)(2,1)} %copy-done.1, bf16[1024,512]{1,0:T(8,128)(2,1)} %collective-permute-done.4.mirror, ...), custom_call_target="tpu_custom_call" | custom-call | tf_op jit(solution)/shard_map/near_0/pallas_call | solution.py:434
  74.3 19.1 %far_0.1 = (bf16[4096,128]{1,0:T(8,128)(2,1)}, f32[4096,128]{1,0:T(8,128)}, f32[4096,128]{1,0:T(8,128)}) custom-call(s32[4]{0:T(128)} %copy-done.9, s32[16]{0:T(128)} %get-tuple-element.34.heads, s32[8320]{0:T(1024)} %get-tuple-element.38.source, s32[8320]{0:T(1024)} %get-tuple-element.37.target, s32[8320]{0:T(1024)} %get-tuple-element.36.rel, ...), custom_call_target="tpu_custom_call" | custom-call | tf_op jit(solution)/shard_map/far_0/pallas_call | solution.py:441
  93.4 2.9 %collective-permute-start.8 = (bf16[1024,512]{1,0:T(8,128)(2,1)}, bf16[1024,512]{1,0:T(8,128)(2,1)S(1)}, u32[]{:S(2)}, u32[]{:S(2)}) collective-permute-start(bf16[1024,512]{1,0:T(8,128)(2,1)} %param.18), channel_id=1, source_target_pairs={{0,0},{1,16},{2,2},{3,18},{4,4},{5,20},{6,6},{7,22},{8,12},{9,28},... | collective-permute-start | bytes 3145736 | tf_op jit(solution)/shard_map/ppermute | solution.py:378
  101.7 13.6 %near_1.1.near = f32[4096,128]{1,0:T(8,128)} custom-call(s32[4]{0:T(128)} %copy-done.9, s32[8320]{0:T(1024)} %get-tuple-element.38.source, s32[8320]{0:T(1024)} %get-tuple-element.37.target, s32[8320]{0:T(1024)} %get-tuple-element.36.rel, bf16[4096,128]{1,0:T(8,128)(2,1)} %get-tuple-element.15.own, bf16[4096,128]{1,0:T(8,128)(2,1)} %copy-done.7, ...), custom_call_target="tpu_custom_call" | custom-call | tf_op jit(solution)/shard_map/near_1/pallas_call | solution.py:434
  115.3 15.5 %collective-permute-done.8.cotangent = bf16[1024,512]{1,0:T(8,128)(2,1)S(1)} collective-permute-done((bf16[1024,512]{1,0:T(8,128)(2,1)}, bf16[1024,512]{1,0:T(8,128)(2,1)S(1)}, u32[]{:S(2)}, u32[]{:S(2)}) %collective-permute-start.8) | collective-permute-done | bytes 1048608 | tf_op jit(solution)/shard_map/ppermute | solution.py:378
  130.8 13.3 %collective-permute-done.6.right = bf16[4096,128]{1,0:T(8,128)(2,1)} collective-permute-done((bf16[4096,128]{1,0:T(8,128)(2,1)}, bf16[4096,128]{1,0:T(8,128)(2,1)}, u32[]{:S(2)}, u32[]{:S(2)}) %collective-permute-start.6) | collective-permute-done | bytes 1048608 | tf_op jit(solution)/shard_map/ppermute | solution.py:378
  144.1 27.4 %far_1.1 = (bf16[1024,512]{1,0:T(8,128)(2,1)}, bf16[4096,128]{1,0:T(8,128)(2,1)}, f32[128,128]{1,0:T(8,128)}, f32[1,128]{1,0:T(1,128)}) custom-call(s32[4]{0:T(128)} %copy-done.9, s32[16]{0:T(128)} %get-tuple-element.34.heads, s32[8320]{0:T(1024)} %get-tuple-element.38.source, s32[8320]{0:T(1024)} %get-tuple-element.37.target, s32[8320]{0:T(1024)} %get-tuple-element.36.rel, ...), custom_call_target="tpu_custom_call" | custom-call | tf_op jit(solution)/shard_map/far_1/pallas_call | solution.py:441
  171.6 8.6 %adjoint_left.1 = bf16[4096,128]{1,0:T(8,128)(2,1)} custom-call(s32[4]{0:T(128)} %copy-done.9, s32[8320]{0:T(1024)} %get-tuple-element.35.source, s32[8320]{0:T(1024)} %get-tuple-element.37.target, s32[8320]{0:T(1024)} %get-tuple-element.36.rel, bf16[4096,128]{1,0:T(8,128)(2,1)} %get-tuple-element.18.grad_mixed, f32[824,128]{1,0:T(8,128)} %copy.34.table), custom_call_target="tpu_custom_call" | custom-call | tf_op jit(solution)/shard_map/adjoint_left/pallas_call | solution.py:459
  180.1 8.8 %adjoint_right.1 = bf16[4096,128]{1,0:T(8,128)(2,1)} custom-call(s32[4]{0:T(128)} %copy-done.9, s32[8320]{0:T(1024)} %get-tuple-element.35.source, s32[8320]{0:T(1024)} %get-tuple-element.37.target, s32[8320]{0:T(1024)} %get-tuple-element.36.rel, bf16[4096,128]{1,0:T(8,128)(2,1)} %get-tuple-element.18.grad_mixed, f32[824,128]{1,0:T(8,128)} %copy.34.table), custom_call_target="tpu_custom_call" | custom-call | tf_op jit(solution)/shard_map/adjoint_right/pallas_call | solution.py:459
  188.9 14.5 %adjoint_near.1 = (f32[4096,128]{1,0:T(8,128)}, bf16[4096,128]{1,0:T(8,128)(2,1)}) custom-call(s32[4]{0:T(128)} %copy-done.9, s32[8320]{0:T(1024)} %get-tuple-element.35.source, s32[8320]{0:T(1024)} %get-tuple-element.37.target, s32[8320]{0:T(1024)} %get-tuple-element.36.rel, bf16[4096,128]{1,0:T(8,128)(2,1)} %get-tuple-element.18.grad_mixed, ...), custom_call_target="tpu_custom_call" | custom-call | tf_op jit(solution)/shard_map/adjoint_near/pallas_call | solution.py:459
  205.4 3.0 %collective-permute-start.9 = (bf16[1024,512]{1,0:T(8,128)(2,1)}, bf16[1024,512]{1,0:T(8,128)(2,1)}, u32[]{:S(2)}, u32[]{:S(2)}) collective-permute-start(bf16[1024,512]{1,0:T(8,128)(2,1)} %get-tuple-element.17), channel_id=1, source_target_pairs={{0,0},{16,1},{2,2},{18,3},{4,4},{20,5},{6,6},{22,7},{12,8},{28,9},... | collective-permute-start | bytes 3145736 | tf_op jit(solution)/shard_map/ppermute | solution.py:378
  208.4 21.2 %collective-permute-done.10.left = bf16[4096,128]{1,0:T(8,128)(2,1)S(1)} collective-permute-done((bf16[4096,128]{1,0:T(8,128)(2,1)}, bf16[4096,128]{1,0:T(8,128)(2,1)S(1)}, u32[]{:S(2)}, u32[]{:S(2)}) %collective-permute-start.10) | collective-permute-done | bytes 1048608 | tf_op jit(solution)/shard_map/ppermute | solution.py:378
  231.5 10.6 %last.1 = f32[72,128]{1,0:T(8,128)} custom-call(bf16[1024,512]{1,0:T(8,128)(2,1)} %copy-done.2, f32[4096,128]{1,0:T(8,128)} %get-tuple-element.19.own, bf16[4096,128]{1,0:T(8,128)(2,1)} %copy-done.5, bf16[4096,128]{1,0:T(8,128)(2,1)} %copy-done.6, bf16[4096,128]{1,0:T(8,128)(2,1)} %copy-done.8, f32[4096,128]{1,0:T(8,128)} %get-tuple-element.21.update, ...), custom_call_target="tpu_custom_call" | custom-call | tf_op jit(solution)/shard_map/last/pallas_call | solution.py:471
  245.8 2.4 collective-permute-done.14
  248.3 3.9 %collective-permute-done.15 = f32[72,128]{1,0:T(8,128)S(1)} collective-permute-done((f32[72,128]{1,0:T(8,128)S(1)}, f32[72,128]{1,0:T(8,128)S(1)}, u32[]{:S(2)}, u32[]{:S(2)}) %collective-permute-start.15) | collective-permute-done | bytes 36896 | tf_op jit(solution)/shard_map/ppermute | solution.py:378
  252.2 2.4 collective-permute-start.16
  254.6 1.9 collective-permute-done.16
  256.5 4.0 %collective-permute-start.17 = (f32[72,128]{1,0:T(8,128)S(1)}, f32[72,128]{1,0:T(8,128)S(1)}, u32[]{:S(2)}, u32[]{:S(2)}) collective-permute-start(f32[72,128]{1,0:T(8,128)S(1)} %add.150), channel_id=1, source_target_pairs={{0,16},{1,17},{2,18},{3,19},{4,20},{5,21},{6,22},{7,23},{8,24},{9,... | collective-permute-start | bytes 110600 | tf_op jit(solution)/shard_map/ppermute | solution.py:378
  263.7 2.3 copy.41
  (102 shorter events, 36.9 us)
Async XLA Ops:
  0.6 19.6 %copy-start = (f32[822,32]{0,1:T(8,128)S(1)}, f32[822,32]{0,1:T(8,128)}, u32[]{:S(2)}) copy-start(f32[822,32]{0,1:T(8,128)} %param.14) | copy-start | bytes 315652
  2.5 13.2 %copy-start.11 = (s32[32]{0:T(128)S(1)}, s32[32]{0:T(128)}, u32[]{:S(2)}) copy-start(s32[32]{0:T(128)} %constant.132.clone) | copy-start | bytes 388
  2.5 15.0 %collective-permute-start = (s32[200,128]{1,0:T(8,128)S(1)}, s32[200,128]{1,0:T(8,128)S(1)}, u32[]{:S(2)}, u32[]{:S(2)}) collective-permute-start(s32[200,128]{1,0:T(8,128)S(1)} %pad_bitcast_fusion), channel_id=1, source_target_pairs={{0,0},{1,16},{2,2},{3,18},{4,4},{5,20},{6,6},{7,22},{8,12},{9,28},... | collective-permute-start | bytes 307208 | tf_op jit(solution)/shard_map/ppermute | solution.py:378
  4.9 28.1 %collective-permute-start.1 = (bf16[1024,512]{1,0:T(8,128)(2,1)}, bf16[1024,512]{1,0:T(8,128)(2,1)S(1)}, u32[]{:S(2)}, u32[]{:S(2)}) collective-permute-start(bf16[1024,512]{1,0:T(8,128)(2,1)} %param.10), channel_id=1, source_target_pairs={{0,0},{1,16},{2,2},{3,18},{4,4},{5,20},{6,6},{7,22},{8,12},{9,28},... | collective-permute-start | bytes 3145736 | tf_op jit(solution)/shard_map/ppermute | solution.py:378
  18.9 40.5 %copy-start.9 = (s32[4]{0:T(128)}, s32[4]{0:T(128)S(1)}, u32[]{:S(2)}) copy-start(s32[4]{0:T(128)S(1)} %select_reduce_fusion.1.ends) | copy-start | bytes 52
  33.1 26.3 %copy-start.1 = (bf16[1024,512]{1,0:T(8,128)(2,1)}, bf16[1024,512]{1,0:T(8,128)(2,1)S(1)}, u32[]{:S(2)}) copy-start(bf16[1024,512]{1,0:T(8,128)(2,1)S(1)} %collective-permute-done.1.own) | copy-start | bytes 3145732
  33.1 26.3 %collective-permute-start.4 = (bf16[1024,512]{1,0:T(8,128)(2,1)S(1)}, bf16[1024,512]{1,0:T(8,128)(2,1)}, u32[]{:S(2)}, u32[]{:S(2)}) collective-permute-start(bf16[1024,512]{1,0:T(8,128)(2,1)S(1)} %collective-permute-done.1.own), channel_id=1, source_target_pairs={{0,1},{16,17},{2,3},{18,19},{4,5},{20,21},{6,7},{22,23},{12,13},{2... | collective-permute-start | bytes 3145736 | tf_op jit(solution)/shard_map/ppermute | solution.py:378
  33.1 39.9 %collective-permute-start.3 = (bf16[1024,512]{1,0:T(8,128)(2,1)S(1)}, bf16[1024,512]{1,0:T(8,128)(2,1)S(1)}, u32[]{:S(2)}, u32[]{:S(2)}) collective-permute-start(bf16[1024,512]{1,0:T(8,128)(2,1)S(1)} %collective-permute-done.1.own), channel_id=1, source_target_pairs={{4,0},{20,16},{6,2},{22,18},{12,4},{28,20},{14,6},{30,22},{8,12},{... | collective-permute-start | bytes 3145736 | tf_op jit(solution)/shard_map/ppermute | solution.py:378
  36.0 37.0 %collective-permute-start.2 = (bf16[1024,512]{1,0:T(8,128)(2,1)S(1)}, bf16[1024,512]{1,0:T(8,128)(2,1)S(1)}, u32[]{:S(2)}, u32[]{:S(2)}) collective-permute-start(bf16[1024,512]{1,0:T(8,128)(2,1)S(1)} %collective-permute-done.1.own), channel_id=1, source_target_pairs={{9,0},{25,16},{11,2},{27,18},{0,4},{16,20},{2,6},{18,22},{4,12},{2... | collective-permute-start | bytes 3145736 | tf_op jit(solution)/shard_map/ppermute | solution.py:378
  74.3 24.1 %copy-start.10 = (f32[32]{0:T(128)S(1)}, f32[32]{0:T(128)}, u32[]{:S(2)}) copy-start(f32[32]{0:T(128)} %get-tuple-element.39) | copy-start | bytes 388
  93.4 7.4 %collective-permute-start.7 = (bf16[4096,128]{1,0:T(8,128)(2,1)}, bf16[4096,128]{1,0:T(8,128)(2,1)S(1)}, u32[]{:S(2)}, u32[]{:S(2)}) collective-permute-start(bf16[4096,128]{1,0:T(8,128)(2,1)} %get-tuple-element.15.own), channel_id=1, source_target_pairs={{0,1},{16,17},{2,3},{18,19},{4,5},{20,21},{6,7},{22,23},{12,13},{2... | collective-permute-start | bytes 3145736 | tf_op jit(solution)/shard_map/ppermute | solution.py:378
  93.4 37.4 %collective-permute-start.8 = (bf16[1024,512]{1,0:T(8,128)(2,1)}, bf16[1024,512]{1,0:T(8,128)(2,1)S(1)}, u32[]{:S(2)}, u32[]{:S(2)}) collective-permute-start(bf16[1024,512]{1,0:T(8,128)(2,1)} %param.18), channel_id=1, source_target_pairs={{0,0},{1,16},{2,2},{3,18},{4,4},{5,20},{6,6},{7,22},{8,12},{9,28},... | collective-permute-start | bytes 3145736 | tf_op jit(solution)/shard_map/ppermute | solution.py:378
  96.3 47.8 %collective-permute-start.6 = (bf16[4096,128]{1,0:T(8,128)(2,1)}, bf16[4096,128]{1,0:T(8,128)(2,1)}, u32[]{:S(2)}, u32[]{:S(2)}) collective-permute-start(bf16[4096,128]{1,0:T(8,128)(2,1)} %get-tuple-element.15.own), channel_id=1, source_target_pairs={{4,0},{20,16},{6,2},{22,18},{12,4},{28,20},{14,6},{30,22},{8,12},{... | collective-permute-start | bytes 3145736 | tf_op jit(solution)/shard_map/ppermute | solution.py:378
  97.5 46.6 %collective-permute-start.5 = (bf16[4096,128]{1,0:T(8,128)(2,1)}, bf16[4096,128]{1,0:T(8,128)(2,1)}, u32[]{:S(2)}, u32[]{:S(2)}) collective-permute-start(bf16[4096,128]{1,0:T(8,128)(2,1)} %get-tuple-element.15.own), channel_id=1, source_target_pairs={{9,0},{25,16},{11,2},{27,18},{0,4},{16,20},{2,6},{18,22},{4,12},{2... | collective-permute-start | bytes 3145736 | tf_op jit(solution)/shard_map/ppermute | solution.py:378
  130.8 13.3 %copy-start.2 = (bf16[1024,512]{1,0:T(8,128)(2,1)}, bf16[1024,512]{1,0:T(8,128)(2,1)S(1)}, u32[]{:S(2)}) copy-start(bf16[1024,512]{1,0:T(8,128)(2,1)S(1)} %collective-permute-done.8.cotangent) | copy-start | bytes 3145732
  203.4 26.2 %collective-permute-start.10 = (bf16[4096,128]{1,0:T(8,128)(2,1)}, bf16[4096,128]{1,0:T(8,128)(2,1)S(1)}, u32[]{:S(2)}, u32[]{:S(2)}) collective-permute-start(bf16[4096,128]{1,0:T(8,128)(2,1)} %adjoint_right.1), channel_id=1, source_target_pairs={{9,0},{25,16},{11,2},{27,18},{0,4},{16,20},{2,6},{18,22},{4,12},{2... | collective-permute-start | bytes 3145736 | tf_op jit(solution)/shard_map/ppermute | solution.py:378
  204.5 25.6 %collective-permute-start.11 = (bf16[4096,128]{1,0:T(8,128)(2,1)}, bf16[4096,128]{1,0:T(8,128)(2,1)S(1)}, u32[]{:S(2)}, u32[]{:S(2)}) collective-permute-start(bf16[4096,128]{1,0:T(8,128)(2,1)} %adjoint_left.1), channel_id=1, source_target_pairs={{4,0},{20,16},{6,2},{22,18},{12,4},{28,20},{14,6},{30,22},{8,12},{... | collective-permute-start | bytes 3145736 | tf_op jit(solution)/shard_map/ppermute | solution.py:378
  205.4 24.7 %collective-permute-start.12 = (bf16[4096,128]{1,0:T(8,128)(2,1)}, bf16[4096,128]{1,0:T(8,128)(2,1)S(1)}, u32[]{:S(2)}, u32[]{:S(2)}) collective-permute-start(bf16[4096,128]{1,0:T(8,128)(2,1)} %get-tuple-element.20), channel_id=1, source_target_pairs={{0,1},{16,17},{2,3},{18,19},{4,5},{20,21},{6,7},{22,23},{12,13},{2... | collective-permute-start | bytes 3145736 | tf_op jit(solution)/shard_map/ppermute | solution.py:378
  205.4 55.1 %collective-permute-start.9 = (bf16[1024,512]{1,0:T(8,128)(2,1)}, bf16[1024,512]{1,0:T(8,128)(2,1)}, u32[]{:S(2)}, u32[]{:S(2)}) collective-permute-start(bf16[1024,512]{1,0:T(8,128)(2,1)} %get-tuple-element.17), channel_id=1, source_target_pairs={{0,0},{16,1},{2,2},{18,3},{4,4},{20,5},{6,6},{22,7},{12,8},{28,9},... | collective-permute-start | bytes 3145736 | tf_op jit(solution)/shard_map/ppermute | solution.py:378
  242.1 1.4 collective-permute-start.13
  244.3 4.0 %collective-permute-start.14 = (f32[72,128]{1,0:T(8,128)S(1)}, f32[72,128]{1,0:T(8,128)S(1)}, u32[]{:S(2)}, u32[]{:S(2)}) collective-permute-start(f32[72,128]{1,0:T(8,128)S(1)} %add.147), channel_id=1, source_target_pairs={{0,2},{1,3},{2,0},{3,1},{4,6},{5,7},{6,4},{7,5},{8,10},{9,11},{10,... | collective-permute-start | bytes 110600 | tf_op jit(solution)/shard_map/ppermute | solution.py:378
  248.2 4.0 %collective-permute-start.15 = (f32[72,128]{1,0:T(8,128)S(1)}, f32[72,128]{1,0:T(8,128)S(1)}, u32[]{:S(2)}, u32[]{:S(2)}) collective-permute-start(f32[72,128]{1,0:T(8,128)S(1)} %add.148), channel_id=1, source_target_pairs={{0,4},{1,5},{2,6},{3,7},{4,0},{5,1},{6,2},{7,3},{8,12},{9,13},{10,... | collective-permute-start | bytes 110600 | tf_op jit(solution)/shard_map/ppermute | solution.py:378
  252.2 4.3 %collective-permute-start.16 = (f32[72,128]{1,0:T(8,128)S(1)}, f32[72,128]{1,0:T(8,128)S(1)}, u32[]{:S(2)}, u32[]{:S(2)}) collective-permute-start(f32[72,128]{1,0:T(8,128)S(1)} %add.149), channel_id=1, source_target_pairs={{0,8},{1,9},{2,10},{3,11},{4,12},{5,13},{6,14},{7,15},{8,0},{9,1},... | collective-permute-start | bytes 110600 | tf_op jit(solution)/shard_map/ppermute | solution.py:378
  256.5 6.0 %collective-permute-start.17 = (f32[72,128]{1,0:T(8,128)S(1)}, f32[72,128]{1,0:T(8,128)S(1)}, u32[]{:S(2)}, u32[]{:S(2)}) collective-permute-start(f32[72,128]{1,0:T(8,128)S(1)} %add.150), channel_id=1, source_target_pairs={{0,16},{1,17},{2,18},{3,19},{4,20},{5,21},{6,22},{7,23},{8,24},{9,... | collective-permute-start | bytes 110600 | tf_op jit(solution)/shard_map/ppermute | solution.py:378
  (6 other events, 6.7 us)

commit v2 on v1

v2 whole, which is shorter than its diff:
```python
import functools

import jax
import jax.numpy as jnp
from jax import lax
from jax.experimental import pallas as pl
from jax.experimental.pallas import tpu as pltpu
from jax.sharding import PartitionSpec as P


DIM = 32
LANES = 128
UNROLL = 24
SUMS = 3
CHUNK = 256
AXES = ("node", "query")
HIGHEST = lax.Precision.HIGHEST
SMEM = pl.BlockSpec(memory_space=pltpu.SMEM)
VMEM = pl.BlockSpec(memory_space=pltpu.VMEM)
ANY = pl.BlockSpec(memory_space=pl.ANY)


def silu_slope(values):
    sigma = jax.nn.sigmoid(values)
    return sigma * (1.0 + values * (1.0 - sigma))


class Seats:
    def __init__(self, nodes, queries):
        self.nodes, self.queries = nodes, queries

    def home(self, part, column):
        return part * self.queries + column

    def seat(self, part, column):
        half = self.nodes // 2
        low = part % half
        node = (column & 1) * half + (low ^ (low >> 1))
        return node * self.queries + (column >> 1) * 2 + part // half

    def blocks(self):
        return [(p, c) for p in range(self.nodes) for c in range(self.queries)]

    def gather(self):
        return [(self.home(p, c), self.seat(p, c)) for p, c in self.blocks()]

    def give_back(self):
        return [(target, source) for source, target in self.gather()]

    def shift(self, step):
        return [
            (self.seat((p - step) % self.nodes, c), self.seat(p, c)) for p, c in self.blocks()
        ]

    def mirror(self):
        return [
            (self.seat(p, c), self.seat((p + self.nodes // 2) % self.nodes, c))
            for p, c in self.blocks()
        ]

    def parts(self):
        table = [0] * (self.nodes * self.queries)
        for p, c in self.blocks():
            table[self.seat(p, c)] = p
        return table


def spread(block_ref, window_ref, first):
    if block_ref.shape[1] == LANES:
        rows = block_ref.shape[0]

        def step(i, carry):
            at = pl.multiple_of(i * CHUNK, CHUNK)
            window_ref[pl.ds(first + at, CHUNK), :] = block_ref[pl.ds(at, CHUNK), :].astype(
                jnp.float32
            )
            return carry

        lax.fori_loop(0, rows // CHUNK, step, 0)
        return
    rows, cols = block_ref.shape
    groups = cols // LANES
    size = CHUNK // groups

    def step(i, carry):
        at = pl.multiple_of(i * size, size)
        for j in range(groups):
            window_ref[pl.ds(first + at * groups + j, size, stride=groups), :] = block_ref[
                pl.ds(at, size), j * LANES : (j + 1) * LANES
            ].astype(jnp.float32)
        return carry

    lax.fori_loop(0, rows // size, step, 0)


def clear(sums):
    def step(i, carry):
        at = pl.multiple_of(i * CHUNK, CHUNK)
        for ref in sums:
            ref[pl.ds(at, CHUNK), :] = jnp.zeros((CHUNK, LANES), jnp.float32)
        return carry

    lax.fori_loop(0, sums[0].shape[0] // CHUNK, step, 0)


def walk(groups, begin, end, from_ref, to_ref, rel_ref, window, table, sums):
    def step(i, carry):
        first = begin + i * UNROLL
        for u in range(UNROLL):
            source = pl.multiple_of(from_ref[first + u], groups)
            target = pl.multiple_of(to_ref[first + u], groups)
            scale = table[pl.ds(rel_ref[first + u], groups, stride=0), :]
            sums[u % SUMS][pl.ds(target, groups), :] += (
                window[pl.ds(source, groups), :] * scale
            )
        return carry

    lax.fori_loop(0, (end - begin) // UNROLL, step, 0)


def total_of(sums, at):
    value = sums[0][pl.ds(at, CHUNK), :]
    for ref in sums[1:]:
        value = value + ref[pl.ds(at, CHUNK), :]
    return value


def fetch(pairs, sems):
    copies = [pltpu.make_async_copy(src, dst, sems.at[i]) for i, (src, dst) in enumerate(pairs)]
    for copy in copies:
        copy.start()
    return copies


def wait(copies):
    for copy in copies:
        copy.wait()


def bucket_kernel(pos_ref, word_ref, count_ref, out_ref, *, edges, dummy):
    unroll = 32

    def step(i, carry):
        for u in range(unroll):
            out_ref[pos_ref[i * unroll + u]] = word_ref[i * unroll + u]
        return carry

    lax.fori_loop(0, edges // unroll, step, 0)

    def fill(i, carry):
        out_ref[i] = dummy
        return carry

    for k in range(4):
        lax.fori_loop(count_ref[k], count_ref[k + 4], fill, 0)


def split(values):
    high = values.astype(jnp.bfloat16)
    low = (values - high.astype(jnp.float32)).astype(jnp.bfloat16)
    return jnp.concatenate([high, low], axis=1)


def split_weight(weight):
    wide = split(weight)
    return jnp.concatenate([wide, wide], axis=0)


def times(values, wide):
    both = jnp.dot(split(values), wide, preferred_element_type=jnp.float32)
    return both[:, :LANES] + both[:, LANES:]


def outer(left, right):
    return lax.dot_general(
        split(left), split(right), (((0,), (0,)), ((), ())), preferred_element_type=jnp.float32
    )


def quarters(wide):
    return (
        wide[:LANES, :LANES] + wide[LANES:, :LANES] + wide[:LANES, LANES:] + wide[LANES:, LANES:]
    )


def near_kernel(
    groups, ends, source, target, rel, own, mirror, table, out,
    source_buf, target_buf, rel_buf, own_buf, mirror_buf, table_buf, window, sems, *sums,
):
    long = sums[0].shape[0]
    states = fetch([(own, own_buf), (mirror, mirror_buf)], sems)
    lists = fetch(
        [(source, source_buf), (target, target_buf), (rel, rel_buf), (table, table_buf)],
        sems.at[pl.ds(2, 4)],
    )
    clear(sums)
    states[0].wait()
    spread(own_buf, window, 0)
    states[1].wait()
    spread(mirror_buf, window, long)
    wait(lists)
    walk(groups, 0, ends[1], source_buf, target_buf, rel_buf, window, table_buf, sums)
    parts = 4
    size = long // parts
    stores = []
    for k in range(parts):

        def step(i, carry):
            at = pl.multiple_of(k * size + i * CHUNK, CHUNK)
            sums[0][pl.ds(at, CHUNK), :] = total_of(sums, at)
            return carry

        lax.fori_loop(0, size // CHUNK, step, 0)
        piece = pl.ds(k * size, size)
        stores += fetch([(sums[0].at[piece, :], out.at[piece, :])], sems.at[pl.ds(6 + k, 1)])
    wait(stores)


def add_boundary(groups, heads, head_rows, ref, long):
    for q in range(head_rows.shape[0]):
        row = heads[q]

        @pl.when((row >= 0) & (row < long // groups))
        def _():
            at = row * groups + q * DIM // LANES
            ref[pl.ds(at, 1), :] += head_rows[q : q + 1, :]


def far_sums(groups, long, ends, heads, inputs, bufs, head_rows, window, sems, sums):
    source, target, rel, left, right, near, table = inputs
    source_buf, target_buf, rel_buf, left_buf, right_buf, table_buf = bufs
    states = fetch(
        [(left, left_buf), (right, right_buf), (near, sums[0].at[pl.ds(0, long), :])], sems
    )
    lists = fetch(
        [(source, source_buf), (target, target_buf), (rel, rel_buf), (table, table_buf)],
        sems.at[pl.ds(3, 4)],
    )
    clear([ref.at[pl.ds(0, long), :] for ref in sums[1:]])
    states[0].wait()
    spread(left_buf, window, 0)
    states[1].wait()
    spread(right_buf, window, long)
    states[2].wait()
    add_boundary(groups, heads, head_rows, sums[0], long)
    wait(lists)
    walk(groups, ends[1], ends[3], source_buf, target_buf, rel_buf, window, table_buf, sums)


def first_kernel(
    groups, ends, heads, head_rows, weight, bias, source, target, rel, left, right, near, table, own,
    state, mixed, update,
    source_buf, target_buf, rel_buf, left_buf, right_buf, table_buf, own_buf, window, mixed_buf,
    update_buf, state_buf, sems, *sums,
):
    long = sums[0].shape[0]
    extra = fetch([(own, own_buf)], sems.at[pl.ds(7, 1)])
    far_sums(
        groups, long, ends, heads, (source, target, rel, left, right, near, table),
        (source_buf, target_buf, rel_buf, left_buf, right_buf, table_buf), head_rows, window, sems,
        sums,
    )
    wait(extra)
    spread(own_buf, window, 0)
    wide = split_weight(weight[...])
    parts = 4
    size = long // parts
    stores = []
    for k in range(parts):

        def step(i, carry):
            rows = pl.ds(pl.multiple_of(k * size + i * CHUNK, CHUNK), CHUNK)
            mix = total_of(sums, pl.multiple_of(k * size + i * CHUNK, CHUNK))
            values = times(mix, wide) + bias[...]
            mixed_buf[rows, :] = mix
            update_buf[rows, :] = values
            state_buf[rows, :] = (window[rows, :] + values * jax.nn.sigmoid(values)).astype(
                jnp.bfloat16
            )
            return carry

        lax.fori_loop(0, size // CHUNK, step, 0)
        rows = pl.ds(k * size, size)
        stores += fetch(
            [
                (state_buf.at[rows, :], state.at[rows, :]),
                (mixed_buf.at[rows, :], mixed.at[rows, :]),
                (update_buf.at[rows, :], update.at[rows, :]),
            ],
            sems.at[pl.ds(8 + 3 * k, 3)],
        )
    wait(stores)


def second_kernel(
    groups, ends, heads, head_rows, weight, bias, weight_back, source, target, rel, left, right, near,
    table, own, cotangent,
    state, grad_mixed, mixed, grad, to_left, to_right,
    source_buf, target_buf, rel_buf, left_buf, right_buf, table_buf, own_buf, cotangent_buf, window,
    mixed_buf, grad_buf, grad_mixed_buf, state_buf, left_out, right_out, sems, *sums,
):
    long = window.shape[0] // 2
    extra = fetch([(own, own_buf), (cotangent, cotangent_buf)], sems.at[pl.ds(7, 2)])
    far_sums(
        groups, long, ends, heads, (source, target, rel, left, right, near, table),
        (source_buf, target_buf, rel_buf, left_buf, right_buf, table_buf), head_rows, window, sems,
        sums,
    )
    wait(extra)
    spread(own_buf, window, 0)
    spread(cotangent_buf, window, long)
    wide = split_weight(weight[...])
    wide_back = split_weight(weight_back[...])

    def step(i, carry):
        at = pl.multiple_of(i * CHUNK, CHUNK)
        rows = pl.ds(at, CHUNK)
        mix = total_of(sums, at)
        values = times(mix, wide) + bias[...]
        sigma = jax.nn.sigmoid(values)
        window[rows, :] += values * sigma
        behind = pl.ds(long + at, CHUNK)
        slope = window[behind, :] * (sigma * (1.0 + values * (1.0 - sigma)))
        back = times(slope, wide_back).astype(jnp.bfloat16)
        mixed_buf[rows, :] = mix
        grad_buf[rows, :] = slope
        grad_mixed_buf[rows, :] = back
        window[behind, :] = back.astype(jnp.float32)
        for ref in sums:
            ref[rows, :] = jnp.zeros((CHUNK, LANES), jnp.float32)
            ref[behind, :] = jnp.zeros((CHUNK, LANES), jnp.float32)
        return carry

    lax.fori_loop(0, long // CHUNK, step, 0)
    size = CHUNK // groups

    def store(i, carry):
        at = pl.multiple_of(i * size, size)
        for j in range(groups):
            state_buf[pl.ds(at, size), j * LANES : (j + 1) * LANES] = window[
                pl.ds(at * groups + j, size, stride=groups), :
            ].astype(jnp.bfloat16)
        return carry

    lax.fori_loop(0, long // CHUNK, store, 0)
    stores = fetch(
        [(state_buf, state), (grad_mixed_buf, grad_mixed), (mixed_buf, mixed), (grad_buf, grad)],
        sems.at[pl.ds(9, 4)],
    )
    walk(
        groups, ends[1], ends[3], target_buf, source_buf, rel_buf, window.at[pl.ds(long, long), :],
        table_buf, sums,
    )

    for k, (buf, out) in enumerate(((left_out, to_left), (right_out, to_right))):

        def total(i, carry):
            at = pl.multiple_of(i * CHUNK, CHUNK)
            buf[pl.ds(at, CHUNK), :] = total_of(sums, k * long + at).astype(jnp.bfloat16)
            return carry

        lax.fori_loop(0, long // CHUNK, total, 0)
        stores += fetch([(buf, out)], sems.at[pl.ds(13 + k, 1)])
    wait(stores)


def adjoint_kernel(
    groups, ends, source, target, rel, grad_mixed, table, cotangent, mixed, grad,
    base, to_mirror, weight_sum, bias_sum,
    source_buf, target_buf, rel_buf, grad_mixed_buf, table_buf, cotangent_buf, mixed_buf, grad_buf,
    mirror_out, window, wide_sum, sems, *sums,
):
    long = window.shape[0]
    loads = fetch([(grad_mixed, grad_mixed_buf)], sems)
    lists = fetch(
        [(source, source_buf), (target, target_buf), (rel, rel_buf), (table, table_buf)],
        sems.at[pl.ds(1, 4)],
    )
    late = fetch(
        [(cotangent, cotangent_buf), (mixed, mixed_buf), (grad, grad_buf)], sems.at[pl.ds(5, 3)]
    )
    clear(sums)
    wait(loads)
    spread(grad_mixed_buf, window, 0)
    wait(lists)
    walk(groups, 0, ends[1], target_buf, source_buf, rel_buf, window, table_buf, sums)

    def total(i, carry):
        at = pl.multiple_of(i * CHUNK, CHUNK)
        mirror_out[pl.ds(at, CHUNK), :] = total_of(sums, long + at).astype(jnp.bfloat16)
        return carry

    lax.fori_loop(0, long // CHUNK, total, 0)
    stores = fetch([(mirror_out, to_mirror)], sems.at[pl.ds(8, 1)])
    wait(late)
    spread(cotangent_buf, window, 0)
    wide_sum[...] = jnp.zeros_like(wide_sum)
    bias_sum[...] = jnp.zeros_like(bias_sum)

    def step(i, carry):
        at = pl.multiple_of(i * CHUNK, CHUNK)
        rows = pl.ds(at, CHUNK)
        window[rows, :] += total_of(sums, at)
        values = grad_buf[rows, :]
        wide_sum[...] += outer(mixed_buf[rows, :], values)
        bias_sum[...] += jnp.sum(values, axis=0, keepdims=True)
        return carry

    lax.fori_loop(0, long // CHUNK, step, 0)
    stores += fetch([(window, base)], sems.at[pl.ds(9, 1)])
    weight_sum[...] = quarters(wide_sum[...])
    wait(stores)


def folded(wide):
    value = wide[:DIM, :DIM]
    for g in range(1, LANES // DIM):
        value = value + wide[g * DIM : (g + 1) * DIM, g * DIM : (g + 1) * DIM]
    return value


def folded_row(wide):
    value = wide[:, :DIM]
    for g in range(1, LANES // DIM):
        value = value + wide[:, g * DIM : (g + 1) * DIM]
    return value


def last_kernel(
    base, left, right, mirror, update, mixed, weight_one, bias_one, out, wide_sum, bias_sum
):
    @pl.when(pl.program_id(0) == 0)
    def _():
        wide_sum[...] = jnp.zeros_like(wide_sum)
        bias_sum[...] = jnp.zeros_like(bias_sum)

    state_grad = base[...]
    for ref in (left, right, mirror):
        state_grad = state_grad + ref[...].astype(jnp.float32)
    grad = state_grad * silu_slope(update[...])
    wide_sum[...] += outer(mixed[...], grad)
    bias_sum[...] += jnp.sum(grad, axis=0, keepdims=True)

    @pl.when(pl.program_id(0) == pl.num_programs(0) - 1)
    def _():
        out[...] = jnp.zeros_like(out)
        out[0:DIM, 0:DIM] = folded(quarters(wide_sum[...]))
        out[DIM : 2 * DIM, 0:DIM] = folded(weight_one[...])
        out[2 * DIM : 2 * DIM + 1, 0:DIM] = folded_row(bias_sum[...])
        out[2 * DIM + 1 : 2 * DIM + 2, 0:DIM] = folded_row(bias_one[...])


def edge_lists(edges, row_count, groups, rel_count):
    tile_count, slot_total = edges.shape[0], edges.shape[2]
    edge_count = tile_count * slot_total
    lines = edge_count // LANES
    slots = edges[:, 0, :].reshape(lines, LANES)
    rows = (edges[:, 1, :] + 64 * lax.iota(jnp.int32, tile_count)[:, None]).reshape(lines, LANES)
    rels = edges[:, 2, :].reshape(lines, LANES)
    quarter = slots // row_count
    local = slots % row_count
    kind = jnp.where(
        quarter == 1, 0, jnp.where(quarter == 3, 1, jnp.where(quarter == 0, 2, 3))
    )
    row_bits = (row_count - 1).bit_length()
    word = (rels << (2 * row_bits + 1)) | (rows << (row_bits + 1)) | ((kind & 1) * row_count + local)
    onehot = (kind[None] == lax.iota(jnp.int32, 4)[:, None, None]).astype(jnp.bfloat16)
    upto = (lax.iota(jnp.int32, LANES)[:, None] <= lax.iota(jnp.int32, LANES)[None, :]).astype(
        jnp.bfloat16
    )
    within = jnp.einsum("krl,lm->krm", onehot, upto, preferred_element_type=jnp.float32)
    per_line = within[:, :, -1]
    above = (lax.iota(jnp.int32, lines)[:, None] > lax.iota(jnp.int32, lines)[None, :]).astype(
        jnp.bfloat16
    )
    before = jnp.einsum(
        "rs,ks->kr", above, per_line.astype(jnp.bfloat16), preferred_element_type=jnp.float32
    )
    counts = jnp.sum(per_line, axis=1).astype(jnp.int32)
    padded = (counts + UNROLL - 1) // UNROLL * UNROLL
    ends = jnp.sum(
        jnp.where(lax.iota(jnp.int32, 4)[:, None] >= lax.iota(jnp.int32, 4)[None, :], padded[None], 0),
        axis=1,
    )
    begins = ends - padded
    place = begins.astype(jnp.float32)[:, None, None] + before[:, :, None] + within - 1.0
    pos = jnp.sum(jnp.where(onehot > 0, place, 0.0), axis=0).astype(jnp.int32)
    room = (edge_count + 4 * UNROLL + LANES - 1) // LANES * LANES
    words = pl.pallas_call(
        functools.partial(bucket_kernel, edges=edge_count, dummy=rel_count << (2 * row_bits + 1)),
        out_shape=jax.ShapeDtypeStruct((room,), jnp.int32),
        in_specs=[SMEM] * 3,
        out_specs=SMEM,
        name="bucket",
    )(pos.reshape(-1), word.reshape(-1), jnp.concatenate([begins + counts, ends]))
    source = (words & (2 * row_count - 1)) * groups
    target = ((words >> (row_bits + 1)) & (row_count - 1)) * groups
    return ends, source, target, words >> (2 * row_bits + 1)


def body(
    entity_state,
    edge_tiles,
    query_head,
    query_relation,
    query_table,
    rel_vectors,
    mix_weight,
    mix_bias,
    cotangent,
):
    row_count, col_count = entity_state.shape
    groups = col_count // LANES
    long = row_count * groups
    query_count = query_head.shape[0]
    rel_count = rel_vectors.shape[1]
    seats = Seats(lax.axis_size("node"), lax.axis_size("query"))

    def send(block, route):
        return lax.ppermute(block, AXES, route)

    def run(fn, args, specs, outs, out_specs, scratch):
        return pl.pallas_call(
            fn, out_shape=outs, in_specs=specs, out_specs=out_specs, scratch_shapes=scratch,
        )(*args)

    wide_f32 = jax.ShapeDtypeStruct((long, LANES), jnp.float32)
    wide_bf16 = jax.ShapeDtypeStruct((long, LANES), jnp.bfloat16)
    f32_buf = pltpu.VMEM((long, LANES), jnp.float32)
    bf16_buf = pltpu.VMEM((long, LANES), jnp.bfloat16)
    pair = pltpu.VMEM((2 * long, LANES), jnp.float32)
    sums = [f32_buf] * SUMS
    pair_sums = [pair] * SUMS
    square = jax.ShapeDtypeStruct((LANES, LANES), jnp.float32)
    line = jax.ShapeDtypeStruct((1, LANES), jnp.float32)

    state_zero = send(entity_state, seats.gather())
    flat = jnp.concatenate([edge_tiles.reshape(-1), query_head, query_relation])
    edge_total = edge_tiles.size
    flat = jnp.pad(flat, (0, -flat.shape[0] % (8 * LANES))).reshape(-1, LANES)
    flat = send(flat, seats.gather()).reshape(-1)
    edges = flat[:edge_total].reshape(edge_tiles.shape)
    own_head = flat[edge_total : edge_total + query_count]
    own_relation = flat[edge_total + query_count : edge_total + 2 * query_count]
    grad_out = send(cotangent, seats.gather())

    linear = lax.axis_index("node") * seats.queries + lax.axis_index("query")
    part = jnp.array(seats.parts(), jnp.int32)[linear]
    heads = own_head - part * row_count
    choose_rel = (own_relation[:, None] == lax.iota(jnp.int32, query_table.shape[0])[None, :]).astype(
        jnp.float32
    )
    query_vec = (
        jnp.dot(choose_rel, query_table, precision=HIGHEST, preferred_element_type=jnp.float32)
        .astype(jnp.bfloat16)
        .astype(jnp.float32)
    )
    repeat = LANES // DIM
    lane_group = lax.iota(jnp.int32, LANES) // DIM
    head_rows = jnp.where(
        lane_group[None, :] == (lax.iota(jnp.int32, query_count) % repeat)[:, None],
        jnp.tile(query_vec, (1, repeat)),
        0.0,
    )
    tables = jnp.tile(jnp.pad(rel_vectors, ((0, 0), (0, -rel_count % 8 or 8), (0, 0))), (1, 1, repeat))
    same = lane_group[:, None] == lane_group[None, :]
    weights = jnp.where(same[None], jnp.tile(mix_weight, (1, repeat, repeat)), 0.0)
    weight_back = weights[1].T
    biases = jnp.tile(mix_bias, (1, repeat))[:, None, :]
    ends, source, target, rel = edge_lists(edges, row_count, groups, rel_count)
    lists = [source, target, rel]
    list_bufs = [pltpu.SMEM(source.shape, jnp.int32)] * 3
    table_buf = pltpu.VMEM(tables.shape[1:], jnp.float32)

    def sems(count):
        return pltpu.SemaphoreType.DMA((count,))

    def halo(state, index):
        buf = pltpu.VMEM(state.shape, jnp.bfloat16)
        mirror = send(state, seats.mirror())
        left = send(state, seats.shift(1))
        right = send(state, seats.shift(-1))
        near = run(
            functools.partial(near_kernel, groups),
            [ends, *lists, state, mirror, tables[index]],
            [SMEM] + [ANY] * 6,
            wide_f32,
            ANY,
            [*list_bufs, buf, buf, table_buf, pair, sems(10), *sums],
        )
        return left, right, near

    left, right, near = halo(state_zero, 0)
    block_buf = pltpu.VMEM(state_zero.shape, jnp.bfloat16)
    state_one, mixed_zero, update_zero = run(
        functools.partial(first_kernel, groups),
        [ends, heads, head_rows, weights[0], biases[0], *lists, left, right, near, tables[0], state_zero],
        [SMEM] * 2 + [VMEM] * 3 + [ANY] * 8,
        [wide_bf16, wide_f32, wide_f32],
        [ANY] * 3,
        [*list_bufs, block_buf, block_buf, table_buf, block_buf, pair, f32_buf, f32_buf, bf16_buf, sems(20)]
        + sums,
    )
    left, right, near = halo(state_one, 1)
    state_two, grad_mixed, mixed_one, grad_one, to_left, to_right = run(
        functools.partial(second_kernel, groups),
        [ends, heads, head_rows, weights[1], biases[1], weight_back, *lists, left, right, near, tables[1]]
        + [state_one, grad_out],
        [SMEM] * 2 + [VMEM] * 4 + [ANY] * 9,
        [jax.ShapeDtypeStruct(entity_state.shape, jnp.bfloat16), wide_bf16, wide_f32, wide_f32]
        + [wide_bf16] * 2,
        [ANY] * 6,
        [*list_bufs, bf16_buf, bf16_buf, table_buf, bf16_buf, block_buf, pair, f32_buf, f32_buf, bf16_buf]
        + [block_buf, bf16_buf, bf16_buf, sems(15), *pair_sums],
    )
    from_right = send(to_left, seats.shift(-1))
    from_left = send(to_right, seats.shift(1))
    final_state = send(state_two, seats.give_back())
    base, to_mirror, weight_one, bias_one = run(
        functools.partial(adjoint_kernel, groups),
        [ends, *lists, grad_mixed, tables[1], grad_out, mixed_one, grad_one],
        [SMEM] + [ANY] * 8,
        [wide_f32, wide_bf16, square, line],
        [ANY] * 2 + [VMEM] * 2,
        [*list_bufs, bf16_buf, table_buf, block_buf, f32_buf, f32_buf, bf16_buf, f32_buf]
        + [pltpu.VMEM((2 * LANES, 2 * LANES), jnp.float32), sems(10), *pair_sums],
    )
    from_mirror = send(to_mirror, seats.mirror())
    steps = 8
    rows = pl.BlockSpec((long // steps, LANES), lambda i: (i, 0))
    whole = lambda shape: pl.BlockSpec(shape, lambda i: (0, 0))
    grads = pl.pallas_call(
        last_kernel,
        out_shape=jax.ShapeDtypeStruct((2 * DIM + 8, LANES), jnp.float32),
        grid=(steps,),
        in_specs=[rows] * 6 + [whole((LANES, LANES)), whole((1, LANES))],
        out_specs=whole((2 * DIM + 8, LANES)),
        scratch_shapes=[
            pltpu.VMEM((2 * LANES, 2 * LANES), jnp.float32),
            pltpu.VMEM((1, LANES), jnp.float32),
        ],
        name="last",
    )(base, from_left, from_right, from_mirror, update_zero, mixed_zero, weight_one, bias_one)
    devices = seats.nodes * seats.queries
    reach = 1
    while reach < devices:
        grads = grads + send(grads, [(i, i ^ reach) for i in range(devices)])
        reach *= 2
    weight_grads = grads[: 2 * DIM, :DIM].reshape(2, DIM, DIM)
    bias_grads = grads[2 * DIM : 2 * DIM + 2, :DIM]
    return (final_state, weight_grads, bias_grads)


def solution(mesh):
    placed = (
        P("node", "query"),
        P("node", None, None),
        P("query"),
        P("query"),
        P(),
        P(),
        P(),
        P(),
        P("node", "query"),
    )

    return jax.shard_map(
        body, mesh=mesh, in_specs=placed, out_specs=(P("node", "query"), P(), P()), check_vma=False
    )
```

time: 269 us -> 236 us (0.88)
  Pallas kernels: 133 us -> 116 us
  waiting for transfers between devices: 74.7 us -> 61.7 us
  starting transfers between devices: 26.8 us -> 23.1 us
    pallas_call x8 -> x6, Pallas kernels: 116 us -> 99.4 us  [the longest x5 91.4 us: run(): pl.pallas_call(fn, out_shape=outs, in_specs=specs, out_specs=out_specs, s...]
    ppermute x18, waiting for transfers between devices: 74.7 us -> 61.7 us  [send(): return lax.ppermute(block, AXES, route)]
    ppermute x18, starting transfers between devices: 26.8 us -> 23.1 us  [send(): return lax.ppermute(block, AXES, route)]
  transfers between devices with their start and end apart: 18 -> 18, of which waited for: 10 -> 8; matrix products, arithmetic and copies ran while one was open for 8% -> 9% of each run, Pallas kernels for 21% -> 30%
where the time goes in v2:
time: 236 us; the launch traced here: 232 us
  Pallas kernels  116 us (49%)
  waiting for transfers between devices  61.7 us (26%)
  starting transfers between devices  23.1 us (10%)
  local copies, waits for them, and re-layouts  19.6 us (8%)
  other arithmetic  9.86 us (4%)
    pallas_call x5, Pallas kernels, run(): pl.pallas_call(fn, out_shape=outs, in_specs=specs, out_specs=out_specs, s...  91.4 us
    ppermute x18, waiting for transfers between devices, send(): return lax.ppermute(block, AXES, route)  61.7 us
    ppermute x18, starting transfers between devices, send(): return lax.ppermute(block, AXES, route)  23.1 us
    pallas_call x1, Pallas kernels, edge_lists(): pl.pallas_call(functools.partial(bucket_kernel, edges=edge_count, dummy=r...  16.6 us
    unnamed x27, local copies, waits for them, and re-layouts  8.04 us
    pallas_call x1, Pallas kernels, body(): pl.pallas_call(last_kernel, out_shape=jax.ShapeDtypeStruct((2 * DIM + 8,...  8 us
  transfers between devices with their start and end apart: 18, of which 8 were waited for; matrix products, arithmetic and copies ran while one was open for 9% of the time, Pallas kernels for 30%

profile of v2, /device:TPU:10, one launch (start us, length us, event | category | flops | bytes accessed | tf_op | source)
XLA Modules:
  0.0 232.4 jit_solution(7845181093159099409)
XLA Ops:
  2.5 2.4 %collective-permute-start = (s32[200,128]{1,0:T(8,128)S(1)}, s32[200,128]{1,0:T(8,128)S(1)}, u32[]{:S(2)}, u32[]{:S(2)}) collective-permute-start(s32[200,128]{1,0:T(8,128)S(1)} %pad_bitcast_fusion), channel_id=1, source_target_pairs={{0,0},{1,16},{2,2},{3,18},{4,4},{5,20},{6,6},{7,22},{8,12},{9,28},... | collective-permute-start | bytes 307208 | tf_op jit(solution)/shard_map/ppermute | solution.py:520
  4.9 3.4 %collective-permute-start.1 = (bf16[1024,512]{1,0:T(8,128)(2,1)}, bf16[1024,512]{1,0:T(8,128)(2,1)S(1)}, u32[]{:S(2)}, u32[]{:S(2)}) collective-permute-start(bf16[1024,512]{1,0:T(8,128)(2,1)} %param.10), channel_id=1, source_target_pairs={{0,0},{1,16},{2,2},{3,18},{4,4},{5,20},{6,6},{7,22},{8,12},{9,28},... | collective-permute-start | bytes 3145736 | tf_op jit(solution)/shard_map/ppermute | solution.py:520
  8.4 1.3 slice_bitcast_fusion.3
  20.6 12.5 %collective-permute-done.1.own = bf16[1024,512]{1,0:T(8,128)(2,1)S(1)} collective-permute-done((bf16[1024,512]{1,0:T(8,128)(2,1)}, bf16[1024,512]{1,0:T(8,128)(2,1)S(1)}, u32[]{:S(2)}, u32[]{:S(2)}) %collective-permute-start.1) | collective-permute-done | bytes 1048608 | tf_op jit(solution)/shard_map/ppermute | solution.py:520
  33.1 2.9 %collective-permute-start.3 = (bf16[1024,512]{1,0:T(8,128)(2,1)S(1)}, bf16[1024,512]{1,0:T(8,128)(2,1)S(1)}, u32[]{:S(2)}, u32[]{:S(2)}) collective-permute-start(bf16[1024,512]{1,0:T(8,128)(2,1)S(1)} %collective-permute-done.1.own), channel_id=1, source_target_pairs={{4,0},{20,16},{6,2},{22,18},{12,4},{28,20},{14,6},{30,22},{8,12},{... | collective-permute-start | bytes 3145736 | tf_op jit(solution)/shard_map/ppermute | solution.py:520
  38.0 1.5 fusion.11.word_ref
  39.5 16.6 %bucket.1 = s32[8320]{0:T(1024)} custom-call(s32[8192]{0:T(1024)} %convert_bitcast_fusion.pos_ref, s32[8192]{0:T(1024)} %fusion.11.word_ref, s32[8]{0:T(128)} %pad_add_fusion.count_ref), custom_call_target="tpu_custom_call" | custom-call | tf_op jit(solution)/shard_map/bucket/pallas_call | solution.py:489
  57.4 1.4 broadcast_shift-right-arithmetic_fusion
  58.8 13.3 %shard_map.121.near = f32[4096,128]{1,0:T(8,128)} custom-call(s32[4]{0:T(128)} %copy-done.9, s32[8320]{0:T(1024)} %get-tuple-element.41.source, s32[8320]{0:T(1024)} %get-tuple-element.40.target, s32[8320]{0:T(1024)} %get-tuple-element.39.rel, bf16[1024,512]{1,0:T(8,128)(2,1)} %copy-done.1, bf16[1024,512]{1,0:T(8,128)(2,1)} %collective-permute-done.4.mirror, ...), custom_call_target="tpu_custom_call" | custom-call | tf_op jit(solution)/shard_map/pallas_call | solution.py:523
  73.5 16.7 %shard_map.122 = (bf16[4096,128]{1,0:T(8,128)(2,1)}, f32[4096,128]{1,0:T(8,128)}, f32[4096,128]{1,0:T(8,128)}) custom-call(s32[4]{0:T(128)} %copy-done.9, s32[16]{0:T(128)} %get-tuple-element.38.heads, f32[16,128]{1,0:T(8,128)} %compare_select_fusion.head_rows, f32[128,128]{1,0:T(8,128)} %copy.30.weight, f32[1,128]{1,0:T(1,128)} %tile.50.bias, ...), custom_call_target="tpu_custom_call" | custom-call | tf_op jit(solution)/shard_map/pallas_call | solution.py:523
  90.2 2.7 %collective-permute-start.8 = (bf16[1024,512]{1,0:T(8,128)(2,1)}, bf16[1024,512]{1,0:T(8,128)(2,1)S(1)}, u32[]{:S(2)}, u32[]{:S(2)}) collective-permute-start(bf16[1024,512]{1,0:T(8,128)(2,1)} %param.18), channel_id=1, source_target_pairs={{0,0},{1,16},{2,2},{3,18},{4,4},{5,20},{6,6},{7,22},{8,12},{9,28},... | collective-permute-start | bytes 3145736 | tf_op jit(solution)/shard_map/ppermute | solution.py:520
  98.3 13.3 %shard_map.123.near = f32[4096,128]{1,0:T(8,128)} custom-call(s32[4]{0:T(128)} %copy-done.9, s32[8320]{0:T(1024)} %get-tuple-element.41.source, s32[8320]{0:T(1024)} %get-tuple-element.40.target, s32[8320]{0:T(1024)} %get-tuple-element.39.rel, bf16[4096,128]{1,0:T(8,128)(2,1)} %get-tuple-element.16.own, bf16[4096,128]{1,0:T(8,128)(2,1)} %copy-done.7, ...), custom_call_target="tpu_custom_call" | custom-call | tf_op jit(solution)/shard_map/pallas_call | solution.py:523
  111.7 16.2 %collective-permute-done.8.cotangent = bf16[1024,512]{1,0:T(8,128)(2,1)S(1)} collective-permute-done((bf16[1024,512]{1,0:T(8,128)(2,1)}, bf16[1024,512]{1,0:T(8,128)(2,1)S(1)}, u32[]{:S(2)}, u32[]{:S(2)}) %collective-permute-start.8) | collective-permute-done | bytes 1048608 | tf_op jit(solution)/shard_map/ppermute | solution.py:520
  127.9 13.1 %collective-permute-done.6.right = bf16[4096,128]{1,0:T(8,128)(2,1)} collective-permute-done((bf16[4096,128]{1,0:T(8,128)(2,1)}, bf16[4096,128]{1,0:T(8,128)(2,1)}, u32[]{:S(2)}, u32[]{:S(2)}) %collective-permute-start.6) | collective-permute-done | bytes 1048608 | tf_op jit(solution)/shard_map/ppermute | solution.py:520
  141.0 29.7 %shard_map.124 = (bf16[1024,512]{1,0:T(8,128)(2,1)}, bf16[4096,128]{1,0:T(8,128)(2,1)}, f32[4096,128]{1,0:T(8,128)}, f32[4096,128]{1,0:T(8,128)}, bf16[4096,128]{1,0:T(8,128)(2,1)}, /*index=5*/bf16[4096,128]{1,0:T(8,128)(2,1)}) custom-call(s32[4]{0:T(128)} %copy-done.9, s32[16]{0:T(128)} %get-tuple-element.38.heads, f32[16,128]{1,0:T(8,128)} %compare_select_fusion.head_rows, ...), custom_call_target="tpu_custom_call" | custom-call | tf_op jit(solution)/shard_map/pallas_call | solution.py:523
  172.8 18.4 %shard_map.125 = (f32[4096,128]{1,0:T(8,128)}, bf16[4096,128]{1,0:T(8,128)(2,1)}, f32[128,128]{1,0:T(8,128)}, f32[1,128]{1,0:T(1,128)}) custom-call(s32[4]{0:T(128)} %copy-done.9, s32[8320]{0:T(1024)} %get-tuple-element.41.source, s32[8320]{0:T(1024)} %get-tuple-element.40.target, s32[8320]{0:T(1024)} %get-tuple-element.39.rel, ...), custom_call_target="tpu_custom_call" | custom-call | tf_op jit(solution)/shard_map/pallas_call | solution.py:523
  191.2 2.8 %collective-permute-start.9 = (bf16[1024,512]{1,0:T(8,128)(2,1)}, bf16[1024,512]{1,0:T(8,128)(2,1)}, u32[]{:S(2)}, u32[]{:S(2)}) collective-permute-start(bf16[1024,512]{1,0:T(8,128)(2,1)} %get-tuple-element.17), channel_id=1, source_target_pairs={{0,0},{16,1},{2,2},{18,3},{4,4},{20,5},{6,6},{22,7},{12,8},{28,9},... | collective-permute-start | bytes 3145736 | tf_op jit(solution)/shard_map/ppermute | solution.py:520
  195.7 8.0 %last.1 = f32[72,128]{1,0:T(8,128)} custom-call(f32[4096,128]{1,0:T(8,128)} %get-tuple-element.21.base, bf16[4096,128]{1,0:T(8,128)(2,1)} %copy-done.5, bf16[4096,128]{1,0:T(8,128)(2,1)} %copy-done.6, bf16[4096,128]{1,0:T(8,128)(2,1)} %copy-done.8, f32[4096,128]{1,0:T(8,128)} %get-tuple-element.25.update, f32[4096,128]{1,0:T(8,128)} %get-tuple-element.26.mixed, ...), custom_call_target="tpu_custom_call" | custom-call | tf_op jit(solution)/shard_map/last/pallas_call | solution.py:632
  205.9 1.5 collective-permute-start.14
  207.4 2.4 %collective-permute-done.14 = f32[72,128]{1,0:T(8,128)S(1)} collective-permute-done((f32[72,128]{1,0:T(8,128)S(1)}, f32[72,128]{1,0:T(8,128)S(1)}, u32[]{:S(2)}, u32[]{:S(2)}) %collective-permute-start.14) | collective-permute-done | bytes 36896 | tf_op jit(solution)/shard_map/ppermute | solution.py:520
  211.1 9.1 %collective-permute-done.15 = f32[72,128]{1,0:T(8,128)S(1)} collective-permute-done((f32[72,128]{1,0:T(8,128)S(1)}, f32[72,128]{1,0:T(8,128)S(1)}, u32[]{:S(2)}, u32[]{:S(2)}) %collective-permute-start.15) | collective-permute-done | bytes 36896 | tf_op jit(solution)/shard_map/ppermute | solution.py:520
  220.7 3.4 %collective-permute-done.16 = f32[72,128]{1,0:T(8,128)S(1)} collective-permute-done((f32[72,128]{1,0:T(8,128)S(1)}, f32[72,128]{1,0:T(8,128)S(1)}, u32[]{:S(2)}, u32[]{:S(2)}) %collective-permute-start.16) | collective-permute-done | bytes 36896 | tf_op jit(solution)/shard_map/ppermute | solution.py:520
  225.2 3.7 %collective-permute-done.17 = f32[72,128]{1,0:T(8,128)S(1)} collective-permute-done((f32[72,128]{1,0:T(8,128)S(1)}, f32[72,128]{1,0:T(8,128)S(1)}, u32[]{:S(2)}, u32[]{:S(2)}) %collective-permute-start.17) | collective-permute-done | bytes 36896 | tf_op jit(solution)/shard_map/ppermute | solution.py:520
  230.2 2.3 copy.37
  (100 shorter events, 32.1 us)
Async XLA Ops:
  0.6 19.7 %copy-start = (f32[822,32]{0,1:T(8,128)S(1)}, f32[822,32]{0,1:T(8,128)}, u32[]{:S(2)}) copy-start(f32[822,32]{0,1:T(8,128)} %param.14) | copy-start | bytes 315652
  2.5 13.3 %copy-start.11 = (s32[32]{0:T(128)S(1)}, s32[32]{0:T(128)}, u32[]{:S(2)}) copy-start(s32[32]{0:T(128)} %constant.118.clone) | copy-start | bytes 388
  2.5 15.0 %collective-permute-start = (s32[200,128]{1,0:T(8,128)S(1)}, s32[200,128]{1,0:T(8,128)S(1)}, u32[]{:S(2)}, u32[]{:S(2)}) collective-permute-start(s32[200,128]{1,0:T(8,128)S(1)} %pad_bitcast_fusion), channel_id=1, source_target_pairs={{0,0},{1,16},{2,2},{3,18},{4,4},{5,20},{6,6},{7,22},{8,12},{9,28},... | collective-permute-start | bytes 307208 | tf_op jit(solution)/shard_map/ppermute | solution.py:520
  4.9 28.1 %collective-permute-start.1 = (bf16[1024,512]{1,0:T(8,128)(2,1)}, bf16[1024,512]{1,0:T(8,128)(2,1)S(1)}, u32[]{:S(2)}, u32[]{:S(2)}) collective-permute-start(bf16[1024,512]{1,0:T(8,128)(2,1)} %param.10), channel_id=1, source_target_pairs={{0,0},{1,16},{2,2},{3,18},{4,4},{5,20},{6,6},{7,22},{8,12},{9,28},... | collective-permute-start | bytes 3145736 | tf_op jit(solution)/shard_map/ppermute | solution.py:520
  18.9 39.9 %copy-start.9 = (s32[4]{0:T(128)}, s32[4]{0:T(128)S(1)}, u32[]{:S(2)}) copy-start(s32[4]{0:T(128)S(1)} %select_reduce_fusion.1.ends) | copy-start | bytes 52
  33.1 25.8 %copy-start.1 = (bf16[1024,512]{1,0:T(8,128)(2,1)}, bf16[1024,512]{1,0:T(8,128)(2,1)S(1)}, u32[]{:S(2)}) copy-start(bf16[1024,512]{1,0:T(8,128)(2,1)S(1)} %collective-permute-done.1.own) | copy-start | bytes 3145732
  33.1 25.8 %collective-permute-start.4 = (bf16[1024,512]{1,0:T(8,128)(2,1)S(1)}, bf16[1024,512]{1,0:T(8,128)(2,1)}, u32[]{:S(2)}, u32[]{:S(2)}) collective-permute-start(bf16[1024,512]{1,0:T(8,128)(2,1)S(1)} %collective-permute-done.1.own), channel_id=1, source_target_pairs={{0,1},{16,17},{2,3},{18,19},{4,5},{20,21},{6,7},{22,23},{12,13},{2... | collective-permute-start | bytes 3145736 | tf_op jit(solution)/shard_map/ppermute | solution.py:520
  33.1 39.1 %collective-permute-start.3 = (bf16[1024,512]{1,0:T(8,128)(2,1)S(1)}, bf16[1024,512]{1,0:T(8,128)(2,1)S(1)}, u32[]{:S(2)}, u32[]{:S(2)}) collective-permute-start(bf16[1024,512]{1,0:T(8,128)(2,1)S(1)} %collective-permute-done.1.own), channel_id=1, source_target_pairs={{4,0},{20,16},{6,2},{22,18},{12,4},{28,20},{14,6},{30,22},{8,12},{... | collective-permute-start | bytes 3145736 | tf_op jit(solution)/shard_map/ppermute | solution.py:520
  36.0 36.1 %collective-permute-start.2 = (bf16[1024,512]{1,0:T(8,128)(2,1)S(1)}, bf16[1024,512]{1,0:T(8,128)(2,1)S(1)}, u32[]{:S(2)}, u32[]{:S(2)}) collective-permute-start(bf16[1024,512]{1,0:T(8,128)(2,1)S(1)} %collective-permute-done.1.own), channel_id=1, source_target_pairs={{9,0},{25,16},{11,2},{27,18},{0,4},{16,20},{2,6},{18,22},{4,12},{2... | collective-permute-start | bytes 3145736 | tf_op jit(solution)/shard_map/ppermute | solution.py:520
  73.5 21.6 %copy-start.10 = (f32[32]{0:T(128)S(1)}, f32[32]{0:T(128)}, u32[]{:S(2)}) copy-start(f32[32]{0:T(128)} %get-tuple-element.43) | copy-start | bytes 388
  90.2 7.2 %collective-permute-start.7 = (bf16[4096,128]{1,0:T(8,128)(2,1)}, bf16[4096,128]{1,0:T(8,128)(2,1)S(1)}, u32[]{:S(2)}, u32[]{:S(2)}) collective-permute-start(bf16[4096,128]{1,0:T(8,128)(2,1)} %get-tuple-element.16.own), channel_id=1, source_target_pairs={{0,1},{16,17},{2,3},{18,19},{4,5},{20,21},{6,7},{22,23},{12,13},{2... | collective-permute-start | bytes 3145736 | tf_op jit(solution)/shard_map/ppermute | solution.py:520
  90.2 37.6 %collective-permute-start.8 = (bf16[1024,512]{1,0:T(8,128)(2,1)}, bf16[1024,512]{1,0:T(8,128)(2,1)S(1)}, u32[]{:S(2)}, u32[]{:S(2)}) collective-permute-start(bf16[1024,512]{1,0:T(8,128)(2,1)} %param.18), channel_id=1, source_target_pairs={{0,0},{1,16},{2,2},{3,18},{4,4},{5,20},{6,6},{7,22},{8,12},{9,28},... | collective-permute-start | bytes 3145736 | tf_op jit(solution)/shard_map/ppermute | solution.py:520
  92.9 48.0 %collective-permute-start.6 = (bf16[4096,128]{1,0:T(8,128)(2,1)}, bf16[4096,128]{1,0:T(8,128)(2,1)}, u32[]{:S(2)}, u32[]{:S(2)}) collective-permute-start(bf16[4096,128]{1,0:T(8,128)(2,1)} %get-tuple-element.16.own), channel_id=1, source_target_pairs={{4,0},{20,16},{6,2},{22,18},{12,4},{28,20},{14,6},{30,22},{8,12},{... | collective-permute-start | bytes 3145736 | tf_op jit(solution)/shard_map/ppermute | solution.py:520
  94.1 46.8 %collective-permute-start.5 = (bf16[4096,128]{1,0:T(8,128)(2,1)}, bf16[4096,128]{1,0:T(8,128)(2,1)}, u32[]{:S(2)}, u32[]{:S(2)}) collective-permute-start(bf16[4096,128]{1,0:T(8,128)(2,1)} %get-tuple-element.16.own), channel_id=1, source_target_pairs={{9,0},{25,16},{11,2},{27,18},{0,4},{16,20},{2,6},{18,22},{4,12},{2... | collective-permute-start | bytes 3145736 | tf_op jit(solution)/shard_map/ppermute | solution.py:520
  127.9 13.1 %copy-start.2 = (bf16[1024,512]{1,0:T(8,128)(2,1)}, bf16[1024,512]{1,0:T(8,128)(2,1)S(1)}, u32[]{:S(2)}) copy-start(bf16[1024,512]{1,0:T(8,128)(2,1)S(1)} %collective-permute-done.8.cotangent) | copy-start | bytes 3145732
  170.7 23.3 %collective-permute-start.10 = (bf16[4096,128]{1,0:T(8,128)(2,1)}, bf16[4096,128]{1,0:T(8,128)(2,1)S(1)}, u32[]{:S(2)}, u32[]{:S(2)}) collective-permute-start(bf16[4096,128]{1,0:T(8,128)(2,1)} %get-tuple-element.22), channel_id=1, source_target_pairs={{9,0},{25,16},{11,2},{27,18},{0,4},{16,20},{2,6},{18,22},{4,12},{2... | collective-permute-start | bytes 3145736 | tf_op jit(solution)/shard_map/ppermute | solution.py:520
  171.7 22.3 %collective-permute-start.11 = (bf16[4096,128]{1,0:T(8,128)(2,1)}, bf16[4096,128]{1,0:T(8,128)(2,1)S(1)}, u32[]{:S(2)}, u32[]{:S(2)}) collective-permute-start(bf16[4096,128]{1,0:T(8,128)(2,1)} %get-tuple-element.23), channel_id=1, source_target_pairs={{4,0},{20,16},{6,2},{22,18},{12,4},{28,20},{14,6},{30,22},{8,12},{... | collective-permute-start | bytes 3145736 | tf_op jit(solution)/shard_map/ppermute | solution.py:520
  191.1 2.9 %collective-permute-start.12 = (bf16[4096,128]{1,0:T(8,128)(2,1)}, bf16[4096,128]{1,0:T(8,128)(2,1)S(1)}, u32[]{:S(2)}, u32[]{:S(2)}) collective-permute-start(bf16[4096,128]{1,0:T(8,128)(2,1)} %get-tuple-element.24), channel_id=1, source_target_pairs={{0,1},{16,17},{2,3},{18,19},{4,5},{20,21},{6,7},{22,23},{12,13},{2... | collective-permute-start | bytes 3145736 | tf_op jit(solution)/shard_map/ppermute | solution.py:520
  191.2 34.0 %collective-permute-start.9 = (bf16[1024,512]{1,0:T(8,128)(2,1)}, bf16[1024,512]{1,0:T(8,128)(2,1)}, u32[]{:S(2)}, u32[]{:S(2)}) collective-permute-start(bf16[1024,512]{1,0:T(8,128)(2,1)} %get-tuple-element.17), channel_id=1, source_target_pairs={{0,0},{16,1},{2,2},{18,3},{4,4},{20,5},{6,6},{22,7},{12,8},{28,9},... | collective-permute-start | bytes 3145736 | tf_op jit(solution)/shard_map/ppermute | solution.py:520
  203.7 1.4 collective-permute-start.13
  205.9 4.0 %collective-permute-start.14 = (f32[72,128]{1,0:T(8,128)S(1)}, f32[72,128]{1,0:T(8,128)S(1)}, u32[]{:S(2)}, u32[]{:S(2)}) collective-permute-start(f32[72,128]{1,0:T(8,128)S(1)} %add.140), channel_id=1, source_target_pairs={{0,2},{1,3},{2,0},{3,1},{4,6},{5,7},{6,4},{7,5},{8,10},{9,11},{10,... | collective-permute-start | bytes 110600 | tf_op jit(solution)/shard_map/ppermute | solution.py:520
  209.9 10.2 %collective-permute-start.15 = (f32[72,128]{1,0:T(8,128)S(1)}, f32[72,128]{1,0:T(8,128)S(1)}, u32[]{:S(2)}, u32[]{:S(2)}) collective-permute-start(f32[72,128]{1,0:T(8,128)S(1)} %add.141), channel_id=1, source_target_pairs={{0,4},{1,5},{2,6},{3,7},{4,0},{5,1},{6,2},{7,3},{8,12},{9,13},{10,... | collective-permute-start | bytes 110600 | tf_op jit(solution)/shard_map/ppermute | solution.py:520
  220.2 4.0 %collective-permute-start.16 = (f32[72,128]{1,0:T(8,128)S(1)}, f32[72,128]{1,0:T(8,128)S(1)}, u32[]{:S(2)}, u32[]{:S(2)}) collective-permute-start(f32[72,128]{1,0:T(8,128)S(1)} %add.142), channel_id=1, source_target_pairs={{0,8},{1,9},{2,10},{3,11},{4,12},{5,13},{6,14},{7,15},{8,0},{9,1},... | collective-permute-start | bytes 110600 | tf_op jit(solution)/shard_map/ppermute | solution.py:520
  224.1 4.9 %collective-permute-start.17 = (f32[72,128]{1,0:T(8,128)S(1)}, f32[72,128]{1,0:T(8,128)S(1)}, u32[]{:S(2)}, u32[]{:S(2)}) collective-permute-start(f32[72,128]{1,0:T(8,128)S(1)} %add.143), channel_id=1, source_target_pairs={{0,16},{1,17},{2,18},{3,19},{4,20},{5,21},{6,22},{7,23},{8,24},{9,... | collective-permute-start | bytes 110600 | tf_op jit(solution)/shard_map/ppermute | solution.py:520
  (6 other events, 7.3 us)

commit v3 on v2

--- a/solution.py
+++ b/solution.py
@@ -47,6 +47,29 @@
     def give_back(self):
         return [(target, source) for source, target in self.gather()]
 
+    def stays(self, part, column):
+        return (column & 1) == part // (self.nodes // 2)
+
+    def shift_from_home(self, step):
+        return [
+            (self.home(p, c), self.seat((p + step) % self.nodes, c))
+            for p, c in self.blocks()
+            if self.stays(p, c)
+        ]
+
+    def shift_from_seat(self, step):
+        return [
+            (self.seat(p, c), self.seat((p + step) % self.nodes, c))
+            for p, c in self.blocks()
+            if not self.stays(p, c)
+        ]
+
+    def near_table(self, step):
+        table = [0] * (self.nodes * self.queries)
+        for p, c in self.blocks():
+            table[self.seat(p, c)] = int(self.stays((p - step) % self.nodes, c))
+        return table
+
     def shift(self, step):
         return [
             (self.seat((p - step) % self.nodes, c), self.seat(p, c)) for p, c in self.blocks()
@@ -104,12 +127,15 @@
 
 
 def walk(groups, begin, end, from_ref, to_ref, rel_ref, window, table, sums):
+    room = from_ref.shape[0] - UNROLL
+    views = [[ref.at[pl.ds(u, room)] for ref in (from_ref, to_ref, rel_ref)] for u in range(UNROLL)]
+
     def step(i, carry):
         first = begin + i * UNROLL
-        for u in range(UNROLL):
-            source = pl.multiple_of(from_ref[first + u], groups)
-            target = pl.multiple_of(to_ref[first + u], groups)
-            scale = table[pl.ds(rel_ref[first + u], groups, stride=0), :]
+        for u, (from_view, to_view, rel_view) in enumerate(views):
+            source = pl.multiple_of(from_view[first], groups)
+            target = pl.multiple_of(to_view[first], groups)
+            scale = table[pl.ds(rel_view[first], groups, stride=0), :]
             sums[u % SUMS][pl.ds(target, groups), :] += (
                 window[pl.ds(source, groups), :] * scale
             )
@@ -137,22 +163,65 @@
         copy.wait()
 
 
-def bucket_kernel(pos_ref, word_ref, count_ref, out_ref, *, edges, dummy):
-    unroll = 32
+def bucket_kernel(
+    edges_ref, out_ref, ends_ref, slots, rows, rels, pos, word, meta, pos_buf, word_buf, meta_buf,
+    sems, *, tile_count, row_count, rel_count,
+):
+    lines = slots.shape[0]
+    deep = lines // tile_count
+    for t in range(tile_count):
+        piece = slice(t * deep, (t + 1) * deep)
+        at = 3 * t * deep
+        slots[piece, :] = edges_ref[at : at + deep, :]
+        rows[piece, :] = edges_ref[at + deep : at + 2 * deep, :] + 64 * t
+        rels[piece, :] = edges_ref[at + 2 * deep : at + 3 * deep, :]
+    slot = slots[...]
+    quarter = sum(((slot >= k * row_count).astype(jnp.int32) for k in range(1, 4)))
+    local = slot - quarter * row_count
+    kind = jnp.where(
+        quarter == 1, 0, jnp.where(quarter == 3, 1, jnp.where(quarter == 0, 2, 3))
+    )
+    second = jnp.where((kind == 1) | (kind == 3), row_count, 0)
+    row_bits = (row_count - 1).bit_length()
+    word[...] = (rels[...] << (2 * row_bits + 1)) | (rows[...] << (row_bits + 1)) | (second + local)
+    shape = (LANES, LANES)
+    upto = (lax.broadcasted_iota(jnp.int32, shape, 0) <= lax.broadcasted_iota(jnp.int32, shape, 1))
+    upto = upto.astype(jnp.float32).astype(jnp.bfloat16)
+    shape = (lines, lines)
+    above = (lax.broadcasted_iota(jnp.int32, shape, 0) > lax.broadcasted_iota(jnp.int32, shape, 1))
+    above = above.astype(jnp.float32).astype(jnp.bfloat16)
+    ones = jnp.ones((LANES, LANES), jnp.bfloat16)
+    place = jnp.zeros((lines, LANES), jnp.float32)
+    begin = jnp.zeros((1, LANES), jnp.float32)
+    for k in range(4):
+        chosen = (kind == k).astype(jnp.float32)
+        onehot = chosen.astype(jnp.bfloat16)
+        within = jnp.dot(onehot, upto, preferred_element_type=jnp.float32)
+        per_line = jnp.dot(onehot, ones, preferred_element_type=jnp.float32)
+        before = jnp.dot(above, per_line.astype(jnp.bfloat16), preferred_element_type=jnp.float32)
+        count = jnp.sum(per_line, axis=0, keepdims=True)
+        place = place + chosen * (begin + before + within - 1.0)
+        meta[k : k + 1, :] = (begin + count).astype(jnp.int32)
+        begin = begin + jnp.floor((count + (UNROLL - 0.5)) / UNROLL) * UNROLL
+        meta[k + 4 : k + 5, :] = begin.astype(jnp.int32)
+    pos[...] = place.astype(jnp.int32)
+    wait(fetch([(pos, pos_buf), (word, word_buf), (meta, meta_buf)], sems))
 
     def step(i, carry):
-        for u in range(unroll):
-            out_ref[pos_ref[i * unroll + u]] = word_ref[i * unroll + u]
-        return carry
-
-    lax.fori_loop(0, edges // unroll, step, 0)
+        for u in range(LANES):
+            out_ref[pos_buf[i, u]] = word_buf[i, u]
+        return carry
+
+    lax.fori_loop(0, lines, step, 0)
+    dummy = rel_count << (2 * row_bits + 1)
 
     def fill(i, carry):
         out_ref[i] = dummy
         return carry
 
     for k in range(4):
-        lax.fori_loop(count_ref[k], count_ref[k + 4], fill, 0)
+        lax.fori_loop(meta_buf[k, 0], meta_buf[k + 4, 0], fill, 0)
+        ends_ref[k] = meta_buf[k + 4, 0]
 
 
 def split(values):
@@ -184,13 +253,13 @@
 
 
 def near_kernel(
-    groups, ends, source, target, rel, own, mirror, table, out,
+    groups, index, ends, source, target, rel, own, mirror, tables, out,
     source_buf, target_buf, rel_buf, own_buf, mirror_buf, table_buf, window, sems, *sums,
 ):
     long = sums[0].shape[0]
     states = fetch([(own, own_buf), (mirror, mirror_buf)], sems)
     lists = fetch(
-        [(source, source_buf), (target, target_buf), (rel, rel_buf), (table, table_buf)],
+        [(source, source_buf), (target, target_buf), (rel, rel_buf), (tables.at[index], table_buf)],
         sems.at[pl.ds(2, 4)],
     )
     clear(sums)
@@ -229,9 +298,20 @@
 def far_sums(groups, long, ends, heads, inputs, bufs, head_rows, window, sems, sums):
     source, target, rel, left, right, near, table = inputs
     source_buf, target_buf, rel_buf, left_buf, right_buf, table_buf = bufs
-    states = fetch(
-        [(left, left_buf), (right, right_buf), (near, sums[0].at[pl.ds(0, long), :])], sems
-    )
+    states = []
+    for k, (sides, buf) in enumerate(((left, left_buf), (right, right_buf))):
+        if isinstance(sides, tuple):
+            flag, early, late = sides
+            for at, ref in ((1, early), (0, late)):
+
+                @pl.when(flag == at)
+                def _():
+                    pltpu.make_async_copy(ref, buf, sems.at[k]).start()
+
+            states.append(pltpu.make_async_copy(early, buf, sems.at[k]))
+        else:
+            states += fetch([(sides, buf)], sems.at[pl.ds(k, 1)])
+    states += fetch([(near, sums[0].at[pl.ds(0, long), :])], sems.at[pl.ds(2, 1)])
     lists = fetch(
         [(source, source_buf), (target, target_buf), (rel, rel_buf), (table, table_buf)],
         sems.at[pl.ds(3, 4)],
@@ -248,21 +328,24 @@
 
 
 def first_kernel(
-    groups, ends, heads, head_rows, weight, bias, source, target, rel, left, right, near, table, own,
-    state, mixed, update,
+    groups, ends, heads, flags, head_rows, weights, biases, source, target, rel, left_early, left_late,
+    right_early, right_late, near, tables, own, state, mixed, update,
     source_buf, target_buf, rel_buf, left_buf, right_buf, table_buf, own_buf, window, mixed_buf,
     update_buf, state_buf, sems, *sums,
 ):
     long = sums[0].shape[0]
     extra = fetch([(own, own_buf)], sems.at[pl.ds(7, 1)])
     far_sums(
-        groups, long, ends, heads, (source, target, rel, left, right, near, table),
+        groups, long, ends, heads,
+        (source, target, rel, (flags[0], left_early, left_late), (flags[1], right_early, right_late))
+        + (near, tables.at[0]),
         (source_buf, target_buf, rel_buf, left_buf, right_buf, table_buf), head_rows, window, sems,
         sums,
     )
     wait(extra)
     spread(own_buf, window, 0)
-    wide = split_weight(weight[...])
+    wide = split_weight(weights[0])
+    bias = biases[0]
     parts = 4
     size = long // parts
     stores = []
@@ -271,7 +354,7 @@
         def step(i, carry):
             rows = pl.ds(pl.multiple_of(k * size + i * CHUNK, CHUNK), CHUNK)
             mix = total_of(sums, pl.multiple_of(k * size + i * CHUNK, CHUNK))
-            values = times(mix, wide) + bias[...]
+            values = times(mix, wide) + bias
             mixed_buf[rows, :] = mix
             update_buf[rows, :] = values
             state_buf[rows, :] = (window[rows, :] + values * jax.nn.sigmoid(values)).astype(
@@ -293,8 +376,8 @@
 
 
 def second_kernel(
-    groups, ends, heads, head_rows, weight, bias, weight_back, source, target, rel, left, right, near,
-    table, own, cotangent,
+    groups, ends, heads, head_rows, weights, biases, source, target, rel, left, right, near, tables, own,
+    cotangent,
     state, grad_mixed, mixed, grad, to_left, to_right,
     source_buf, target_buf, rel_buf, left_buf, right_buf, table_buf, own_buf, cotangent_buf, window,
     mixed_buf, grad_buf, grad_mixed_buf, state_buf, left_out, right_out, sems, *sums,
@@ -302,21 +385,22 @@
     long = window.shape[0] // 2
     extra = fetch([(own, own_buf), (cotangent, cotangent_buf)], sems.at[pl.ds(7, 2)])
     far_sums(
-        groups, long, ends, heads, (source, target, rel, left, right, near, table),
+        groups, long, ends, heads, (source, target, rel, left, right, near, tables.at[1]),
         (source_buf, target_buf, rel_buf, left_buf, right_buf, table_buf), head_rows, window, sems,
         sums,
     )
     wait(extra)
     spread(own_buf, window, 0)
     spread(cotangent_buf, window, long)
-    wide = split_weight(weight[...])
-    wide_back = split_weight(weight_back[...])
+    wide = split_weight(weights[1])
+    wide_back = split_weight(weights[1].T)
+    bias = biases[1]
 
     def step(i, carry):
         at = pl.multiple_of(i * CHUNK, CHUNK)
         rows = pl.ds(at, CHUNK)
         mix = total_of(sums, at)
-        values = times(mix, wide) + bias[...]
+        values = times(mix, wide) + bias
         sigma = jax.nn.sigmoid(values)
         window[rows, :] += values * sigma
         behind = pl.ds(long + at, CHUNK)
@@ -365,7 +449,7 @@
 
 
 def adjoint_kernel(
-    groups, ends, source, target, rel, grad_mixed, table, cotangent, mixed, grad,
+    groups, ends, source, target, rel, grad_mixed, tables, cotangent, mixed, grad,
     base, to_mirror, weight_sum, bias_sum,
     source_buf, target_buf, rel_buf, grad_mixed_buf, table_buf, cotangent_buf, mixed_buf, grad_buf,
     mirror_out, window, wide_sum, sems, *sums,
@@ -373,7 +457,7 @@
     long = window.shape[0]
     loads = fetch([(grad_mixed, grad_mixed_buf)], sems)
     lists = fetch(
-        [(source, source_buf), (target, target_buf), (rel, rel_buf), (table, table_buf)],
+        [(source, source_buf), (target, target_buf), (rel, rel_buf), (tables.at[1], table_buf)],
         sems.at[pl.ds(1, 4)],
     )
     late = fetch(
@@ -450,49 +534,25 @@
         out[2 * DIM + 1 : 2 * DIM + 2, 0:DIM] = folded_row(bias_one[...])
 
 
-def edge_lists(edges, row_count, groups, rel_count):
-    tile_count, slot_total = edges.shape[0], edges.shape[2]
+def edge_lists(edges, tile_count, slot_total, row_count, groups, rel_count):
     edge_count = tile_count * slot_total
     lines = edge_count // LANES
-    slots = edges[:, 0, :].reshape(lines, LANES)
-    rows = (edges[:, 1, :] + 64 * lax.iota(jnp.int32, tile_count)[:, None]).reshape(lines, LANES)
-    rels = edges[:, 2, :].reshape(lines, LANES)
-    quarter = slots // row_count
-    local = slots % row_count
-    kind = jnp.where(
-        quarter == 1, 0, jnp.where(quarter == 3, 1, jnp.where(quarter == 0, 2, 3))
-    )
     row_bits = (row_count - 1).bit_length()
-    word = (rels << (2 * row_bits + 1)) | (rows << (row_bits + 1)) | ((kind & 1) * row_count + local)
-    onehot = (kind[None] == lax.iota(jnp.int32, 4)[:, None, None]).astype(jnp.bfloat16)
-    upto = (lax.iota(jnp.int32, LANES)[:, None] <= lax.iota(jnp.int32, LANES)[None, :]).astype(
-        jnp.bfloat16
-    )
-    within = jnp.einsum("krl,lm->krm", onehot, upto, preferred_element_type=jnp.float32)
-    per_line = within[:, :, -1]
-    above = (lax.iota(jnp.int32, lines)[:, None] > lax.iota(jnp.int32, lines)[None, :]).astype(
-        jnp.bfloat16
-    )
-    before = jnp.einsum(
-        "rs,ks->kr", above, per_line.astype(jnp.bfloat16), preferred_element_type=jnp.float32
-    )
-    counts = jnp.sum(per_line, axis=1).astype(jnp.int32)
-    padded = (counts + UNROLL - 1) // UNROLL * UNROLL
-    ends = jnp.sum(
-        jnp.where(lax.iota(jnp.int32, 4)[:, None] >= lax.iota(jnp.int32, 4)[None, :], padded[None], 0),
-        axis=1,
-    )
-    begins = ends - padded
-    place = begins.astype(jnp.float32)[:, None, None] + before[:, :, None] + within - 1.0
-    pos = jnp.sum(jnp.where(onehot > 0, place, 0.0), axis=0).astype(jnp.int32)
-    room = (edge_count + 4 * UNROLL + LANES - 1) // LANES * LANES
-    words = pl.pallas_call(
-        functools.partial(bucket_kernel, edges=edge_count, dummy=rel_count << (2 * row_bits + 1)),
-        out_shape=jax.ShapeDtypeStruct((room,), jnp.int32),
-        in_specs=[SMEM] * 3,
-        out_specs=SMEM,
+    room = (edge_count + 5 * UNROLL + LANES - 1) // LANES * LANES
+    flat = pltpu.VMEM((lines, LANES), jnp.int32)
+    flat_smem = pltpu.SMEM((lines, LANES), jnp.int32)
+    words, ends = pl.pallas_call(
+        functools.partial(
+            bucket_kernel, tile_count=tile_count, row_count=row_count, rel_count=rel_count
+        ),
+        out_shape=[jax.ShapeDtypeStruct((room,), jnp.int32), jax.ShapeDtypeStruct((4,), jnp.int32)],
+        in_specs=[VMEM],
+        out_specs=[SMEM] * 2,
+        scratch_shapes=[flat] * 5
+        + [pltpu.VMEM((8, LANES), jnp.int32), flat_smem, flat_smem]
+        + [pltpu.SMEM((8, LANES), jnp.int32), pltpu.SemaphoreType.DMA((3,))],
         name="bucket",
-    )(pos.reshape(-1), word.reshape(-1), jnp.concatenate([begins + counts, ends]))
+    )(edges)
     source = (words & (2 * row_count - 1)) * groups
     target = ((words >> (row_bits + 1)) & (row_count - 1)) * groups
     return ends, source, target, words >> (2 * row_bits + 1)
@@ -534,12 +594,14 @@
     square = jax.ShapeDtypeStruct((LANES, LANES), jnp.float32)
     line = jax.ShapeDtypeStruct((1, LANES), jnp.float32)
 
-    state_zero = send(entity_state, seats.gather())
     flat = jnp.concatenate([edge_tiles.reshape(-1), query_head, query_relation])
     edge_total = edge_tiles.size
     flat = jnp.pad(flat, (0, -flat.shape[0] % (8 * LANES))).reshape(-1, LANES)
-    flat = send(flat, seats.gather()).reshape(-1)
-    edges = flat[:edge_total].reshape(edge_tiles.shape)
+    edges = send(flat, seats.gather())
+    flat = edges.reshape(-1)
+    state_zero = send(entity_state, seats.gather())
+    left_early = send(entity_state, seats.shift_from_home(1))
+    right_early = send(entity_state, seats.shift_from_home(-1))
     own_head = flat[edge_total : edge_total + query_count]
     own_relation = flat[edge_total + query_count : edge_total + 2 * query_count]
     grad_out = send(cotangent, seats.gather())
@@ -547,6 +609,7 @@
     linear = lax.axis_index("node") * seats.queries + lax.axis_index("query")
     part = jnp.array(seats.parts(), jnp.int32)[linear]
     heads = own_head - part * row_count
+    flags = jnp.array([seats.near_table(1), seats.near_table(-1)], jnp.int32)[:, linear]
     choose_rel = (own_relation[:, None] == lax.iota(jnp.int32, query_table.shape[0])[None, :]).astype(
         jnp.float32
     )
@@ -565,9 +628,10 @@
     tables = jnp.tile(jnp.pad(rel_vectors, ((0, 0), (0, -rel_count % 8 or 8), (0, 0))), (1, 1, repeat))
     same = lane_group[:, None] == lane_group[None, :]
     weights = jnp.where(same[None], jnp.tile(mix_weight, (1, repeat, repeat)), 0.0)
-    weight_back = weights[1].T
     biases = jnp.tile(mix_bias, (1, repeat))[:, None, :]
-    ends, source, target, rel = edge_lists(edges, row_count, groups, rel_count)
+    ends, source, target, rel = edge_lists(
+        edges, edge_tiles.shape[0], edge_tiles.shape[2], row_count, groups, rel_count
+    )
     lists = [source, target, rel]
     list_bufs = [pltpu.SMEM(source.shape, jnp.int32)] * 3
     table_buf = pltpu.VMEM(tables.shape[1:], jnp.float32)
@@ -578,11 +642,11 @@
     def halo(state, index):
         buf = pltpu.VMEM(state.shape, jnp.bfloat16)
         mirror = send(state, seats.mirror())
-        left = send(state, seats.shift(1))
-        right = send(state, seats.shift(-1))
+        left = send(state, seats.shift(1) if index else seats.shift_from_seat(1))
+        right = send(state, seats.shift(-1) if index else seats.shift_from_seat(-1))
         near = run(
-            functools.partial(near_kernel, groups),
-            [ends, *lists, state, mirror, tables[index]],
+            functools.partial(near_kernel, groups, index),
+            [ends, *lists, state, mirror, tables],
             [SMEM] + [ANY] * 6,
             wide_f32,
             ANY,
@@ -594,8 +658,9 @@
     block_buf = pltpu.VMEM(state_zero.shape, jnp.bfloat16)
     state_one, mixed_zero, update_zero = run(
         functools.partial(first_kernel, groups),
-        [ends, heads, head_rows, weights[0], biases[0], *lists, left, right, near, tables[0], state_zero],
-        [SMEM] * 2 + [VMEM] * 3 + [ANY] * 8,
+        [ends, heads, flags, head_rows, weights, biases, *lists, left_early, left, right_early, right]
+        + [near, tables, state_zero],
+        [SMEM] * 3 + [VMEM] * 3 + [ANY] * 10,
         [wide_bf16, wide_f32, wide_f32],
         [ANY] * 3,
         [*list_bufs, block_buf, block_buf, table_buf, block_buf, pair, f32_buf, f32_buf, bf16_buf, sems(20)]
@@ -604,9 +669,8 @@
     left, right, near = halo(state_one, 1)
     state_two, grad_mixed, mixed_one, grad_one, to_left, to_right = run(
         functools.partial(second_kernel, groups),
-        [ends, heads, head_rows, weights[1], biases[1], weight_back, *lists, left, right, near, tables[1]]
-        + [state_one, grad_out],
-        [SMEM] * 2 + [VMEM] * 4 + [ANY] * 9,
+        [ends, heads, head_rows, weights, biases, *lists, left, right, near, tables, state_one, grad_out],
+        [SMEM] * 2 + [VMEM] * 3 + [ANY] * 9,
         [jax.ShapeDtypeStruct(entity_state.shape, jnp.bfloat16), wide_bf16, wide_f32, wide_f32]
         + [wide_bf16] * 2,
         [ANY] * 6,
@@ -618,7 +682,7 @@
     final_state = send(state_two, seats.give_back())
     base, to_mirror, weight_one, bias_one = run(
         functools.partial(adjoint_kernel, groups),
-        [ends, *lists, grad_mixed, tables[1], grad_out, mixed_one, grad_one],
+        [ends, *lists, grad_mixed, tables, grad_out, mixed_one, grad_one],
         [SMEM] + [ANY] * 8,
         [wide_f32, wide_bf16, square, line],
         [ANY] * 2 + [VMEM] * 2,

time: 236 us -> 235 us (level)
  starting transfers between devices: 23.1 us -> 40 us
  waiting for transfers between devices: 61.7 us -> 54.3 us
  other arithmetic: 9.86 us -> 5 us
  local copies, waits for them, and re-layouts: 19.6 us -> 16.3 us
    ppermute x18 -> x20, starting transfers between devices: 23.1 us -> 40 us  [send(): return lax.ppermute(block, AXES, route)]
    ppermute x18 -> x20, waiting for transfers between devices: 61.7 us -> 54.3 us  [send(): return lax.ppermute(block, AXES, route)]
    unnamed x27 -> x26, local copies, waits for them, and re-layouts: 8.04 us -> 8.05 us
  transfers between devices with their start and end apart: 18 -> 20, of which waited for: 8 -> 9; matrix products, arithmetic and copies ran while one was open for 9% -> 6% of each run, Pallas kernels for 30% -> 30%
where the time goes in v3:
time: 235 us; the launch traced here: 233 us
  Pallas kernels  116 us (49%)
  waiting for transfers between devices  54.3 us (23%)
  starting transfers between devices  40 us (17%)
  local copies, waits for them, and re-layouts  16.3 us (7%)
  other arithmetic  5 us (2%)
    pallas_call x5, Pallas kernels, run(): pl.pallas_call(fn, out_shape=outs, in_specs=specs, out_specs=out_specs, s...  89.9 us
    ppermute x20, waiting for transfers between devices, send(): return lax.ppermute(block, AXES, route)  54.3 us
    ppermute x20, starting transfers between devices, send(): return lax.ppermute(block, AXES, route)  40 us
    pallas_call x1, Pallas kernels, edge_lists(): pl.pallas_call(functools.partial(bucket_kernel, tile_count=tile_count, ro...  17.7 us
    unnamed x26, local copies, waits for them, and re-layouts  8.05 us
    pallas_call x1, Pallas kernels, body(): pl.pallas_call(last_kernel, out_shape=jax.ShapeDtypeStruct((2 * DIM + 8,...  8 us
  transfers between devices with their start and end apart: 20, of which 9 were waited for; matrix products, arithmetic and copies ran while one was open for 6% of the time, Pallas kernels for 30%

profile of v3, /device:TPU:10, one launch (start us, length us, event | category | flops | bytes accessed | tf_op | source)
XLA Modules:
  0.0 232.9 jit_solution(15642182425202727668)
XLA Ops:
  0.7 2.6 %collective-permute-start.2 = (bf16[1024,512]{1,0:T(8,128)(2,1)}, bf16[1024,512]{1,0:T(8,128)(2,1)S(1)}, u32[]{:S(2)}, u32[]{:S(2)}) collective-permute-start(bf16[1024,512]{1,0:T(8,128)(2,1)} %param.11), channel_id=1, source_target_pairs={{0,0},{1,16},{2,2},{3,18},{4,4},{5,20},{6,6},{7,22},{8,12},{9,28},... | collective-permute-start | bytes 3145736 | tf_op jit(solution)/shard_map/ppermute | solution.py:580
  3.2 4.1 %collective-permute-start.1 = (bf16[1024,512]{1,0:T(8,128)(2,1)}, bf16[1024,512]{1,0:T(8,128)(2,1)S(1)}, u32[]{:S(2)}, u32[]{:S(2)}) collective-permute-start(bf16[1024,512]{1,0:T(8,128)(2,1)} %param.11), channel_id=1, source_target_pairs={{0,4},{2,6},{4,12},{6,14},{8,8},{10,10},{12,1},{14,3},{17,21},{19,... | collective-permute-start | bytes 3145736 | tf_op jit(solution)/shard_map/ppermute | solution.py:580
  7.3 9.5 %collective-permute-start.4 = (bf16[1024,512]{1,0:T(8,128)(2,1)}, bf16[1024,512]{1,0:T(8,128)(2,1)}, u32[]{:S(2)}, u32[]{:S(2)}) collective-permute-start(bf16[1024,512]{1,0:T(8,128)(2,1)} %param.11), channel_id=1, source_target_pairs={{0,9},{2,11},{4,0},{6,2},{8,4},{10,6},{12,12},{14,14},{17,24},{19,... | collective-permute-start | bytes 3145736 | tf_op jit(solution)/shard_map/ppermute | solution.py:580
  19.3 1.9 collective-permute-start
  28.1 1.9 collective-permute-done.2.own
  35.1 17.7 %bucket.1 = (s32[8320]{0:T(1024)}, s32[4]{0:T(128)}) custom-call(s32[200,128]{1,0:T(8,128)} %collective-permute-done.edges_ref), custom_call_target="tpu_custom_call" | custom-call | tf_op jit(solution)/shard_map/bucket/pallas_call | solution.py:544
  55.9 13.1 %shard_map.130.near = f32[4096,128]{1,0:T(8,128)} custom-call(s32[4]{0:T(128)} %get-tuple-element.18.ends, s32[8320]{0:T(1024)} %get-tuple-element.37.source, s32[8320]{0:T(1024)} %get-tuple-element.36.target, s32[8320]{0:T(1024)} %get-tuple-element.35.rel, bf16[1024,512]{1,0:T(8,128)(2,1)} %copy-done.2, bf16[1024,512]{1,0:T(8,128)(2,1)} %copy-done.6, ...), custom_call_target="tpu_custom_call" | custom-call | tf_op jit(solution)/shard_map/pallas_call | solution.py:583
  69.9 16.5 %shard_map.131 = (bf16[4096,128]{1,0:T(8,128)(2,1)}, f32[4096,128]{1,0:T(8,128)}, f32[4096,128]{1,0:T(8,128)}) custom-call(s32[4]{0:T(128)} %get-tuple-element.18.ends, s32[16]{0:T(128)} %get-tuple-element.34.heads, s32[2]{0:T(128)} %dynamic-slice_bitcast_fusion.flags, f32[16,128]{1,0:T(8,128)} %compare_select_fusion.head_rows, ...), custom_call_target="tpu_custom_call" | custom-call | tf_op jit(solution)/shard_map/pallas_call | solution.py:583
  86.5 3.3 %collective-permute-start.9 = (bf16[4096,128]{1,0:T(8,128)(2,1)}, bf16[4096,128]{1,0:T(8,128)(2,1)}, u32[]{:S(2)}, u32[]{:S(2)}) collective-permute-start(bf16[4096,128]{1,0:T(8,128)(2,1)} %get-tuple-element.20.own), channel_id=1, source_target_pairs={{0,1},{16,17},{2,3},{18,19},{4,5},{20,21},{6,7},{22,23},{12,13},{2... | collective-permute-start | bytes 3145736 | tf_op jit(solution)/shard_map/ppermute | solution.py:580
  89.7 2.4 %collective-permute-start.10 = (bf16[1024,512]{1,0:T(8,128)(2,1)}, bf16[1024,512]{1,0:T(8,128)(2,1)S(1)}, u32[]{:S(2)}, u32[]{:S(2)}) collective-permute-start(bf16[1024,512]{1,0:T(8,128)(2,1)} %param.19), channel_id=1, source_target_pairs={{0,0},{1,16},{2,2},{3,18},{4,4},{5,20},{6,6},{7,22},{8,12},{9,28},... | collective-permute-start | bytes 3145736 | tf_op jit(solution)/shard_map/ppermute | solution.py:580
  92.2 2.0 collective-permute-start.7
  94.2 13.0 %shard_map.132.near = f32[4096,128]{1,0:T(8,128)} custom-call(s32[4]{0:T(128)} %get-tuple-element.18.ends, s32[8320]{0:T(1024)} %get-tuple-element.37.source, s32[8320]{0:T(1024)} %get-tuple-element.36.target, s32[8320]{0:T(1024)} %get-tuple-element.35.rel, bf16[4096,128]{1,0:T(8,128)(2,1)} %get-tuple-element.20.own, ...), custom_call_target="tpu_custom_call" | custom-call | tf_op jit(solution)/shard_map/pallas_call | solution.py:583
  107.3 20.3 %collective-permute-done.10.cotangent = bf16[1024,512]{1,0:T(8,128)(2,1)S(1)} collective-permute-done((bf16[1024,512]{1,0:T(8,128)(2,1)}, bf16[1024,512]{1,0:T(8,128)(2,1)S(1)}, u32[]{:S(2)}, u32[]{:S(2)}) %collective-permute-start.10) | collective-permute-done | bytes 1048608 | tf_op jit(solution)/shard_map/ppermute | solution.py:580
  127.6 12.8 %collective-permute-done.8.right = bf16[4096,128]{1,0:T(8,128)(2,1)S(1)} collective-permute-done((bf16[4096,128]{1,0:T(8,128)(2,1)}, bf16[4096,128]{1,0:T(8,128)(2,1)S(1)}, u32[]{:S(2)}, u32[]{:S(2)}) %collective-permute-start.8) | collective-permute-done | bytes 1048608 | tf_op jit(solution)/shard_map/ppermute | solution.py:580
  142.3 29.3 %shard_map.133 = (bf16[1024,512]{1,0:T(8,128)(2,1)}, bf16[4096,128]{1,0:T(8,128)(2,1)}, f32[4096,128]{1,0:T(8,128)}, f32[4096,128]{1,0:T(8,128)}, bf16[4096,128]{1,0:T(8,128)(2,1)}, /*index=5*/bf16[4096,128]{1,0:T(8,128)(2,1)}) custom-call(s32[4]{0:T(128)} %get-tuple-element.18.ends, s32[16]{0:T(128)} %get-tuple-element.34.heads, ...), custom_call_target="tpu_custom_call" | custom-call | tf_op jit(solution)/shard_map/pallas_call | solution.py:583
  171.7 2.0 collective-permute-start.13
  173.7 18.0 %shard_map.134 = (f32[4096,128]{1,0:T(8,128)}, bf16[4096,128]{1,0:T(8,128)(2,1)}, f32[128,128]{1,0:T(8,128)}, f32[1,128]{1,0:T(1,128)}) custom-call(s32[4]{0:T(128)} %get-tuple-element.18.ends, s32[8320]{0:T(1024)} %get-tuple-element.37.source, s32[8320]{0:T(1024)} %get-tuple-element.36.target, s32[8320]{0:T(1024)} %get-tuple-element.35.rel, ...), custom_call_target="tpu_custom_call" | custom-call | tf_op jit(solution)/shard_map/pallas_call | solution.py:583
  191.7 1.9 collective-permute-start.11
  195.6 8.0 %last.1 = f32[72,128]{1,0:T(8,128)} custom-call(f32[4096,128]{1,0:T(8,128)} %get-tuple-element.25.base, bf16[4096,128]{1,0:T(8,128)(2,1)} %copy-done.3, bf16[4096,128]{1,0:T(8,128)(2,1)} %copy-done.4, bf16[4096,128]{1,0:T(8,128)(2,1)} %copy-done.5, f32[4096,128]{1,0:T(8,128)} %get-tuple-element.29.update, f32[4096,128]{1,0:T(8,128)} %get-tuple-element.30.mixed, ...), custom_call_target="tpu_custom_call" | custom-call | tf_op jit(solution)/shard_map/last/pallas_call | solution.py:696
  208.3 2.4 %collective-permute-done.16 = f32[72,128]{1,0:T(8,128)S(1)} collective-permute-done((f32[72,128]{1,0:T(8,128)S(1)}, f32[72,128]{1,0:T(8,128)S(1)}, u32[]{:S(2)}, u32[]{:S(2)}) %collective-permute-start.16) | collective-permute-done | bytes 36896 | tf_op jit(solution)/shard_map/ppermute | solution.py:580
  212.6 8.1 %collective-permute-done.17 = f32[72,128]{1,0:T(8,128)S(1)} collective-permute-done((f32[72,128]{1,0:T(8,128)S(1)}, f32[72,128]{1,0:T(8,128)S(1)}, u32[]{:S(2)}, u32[]{:S(2)}) %collective-permute-start.17) | collective-permute-done | bytes 36896 | tf_op jit(solution)/shard_map/ppermute | solution.py:580
  221.1 3.5 %collective-permute-done.18 = f32[72,128]{1,0:T(8,128)S(1)} collective-permute-done((f32[72,128]{1,0:T(8,128)S(1)}, f32[72,128]{1,0:T(8,128)S(1)}, u32[]{:S(2)}, u32[]{:S(2)}) %collective-permute-start.18) | collective-permute-done | bytes 36896 | tf_op jit(solution)/shard_map/ppermute | solution.py:580
  226.2 3.3 %collective-permute-done.19 = f32[72,128]{1,0:T(8,128)S(1)} collective-permute-done((f32[72,128]{1,0:T(8,128)S(1)}, f32[72,128]{1,0:T(8,128)S(1)}, u32[]{:S(2)}, u32[]{:S(2)}) %collective-permute-start.19) | collective-permute-done | bytes 36896 | tf_op jit(solution)/shard_map/ppermute | solution.py:580
  230.7 2.3 copy.22
  (78 shorter events, 31.5 us)
Async XLA Ops:
  0.6 34.1 %copy-start = (f32[822,32]{0,1:T(8,128)S(1)}, f32[822,32]{0,1:T(8,128)}, u32[]{:S(2)}) copy-start(f32[822,32]{0,1:T(8,128)} %param.15) | copy-start | bytes 315652
  0.6 23.0 %copy-start.10 = (f32[2,822,32]{1,2,0:T(8,128)S(1)}, f32[2,822,32]{1,2,0:T(8,128)}, u32[]{:S(2)}) copy-start(f32[2,822,32]{1,2,0:T(8,128)} %param.16) | copy-start | bytes 631300
  0.7 29.4 %collective-permute-start.2 = (bf16[1024,512]{1,0:T(8,128)(2,1)}, bf16[1024,512]{1,0:T(8,128)(2,1)S(1)}, u32[]{:S(2)}, u32[]{:S(2)}) collective-permute-start(bf16[1024,512]{1,0:T(8,128)(2,1)} %param.11), channel_id=1, source_target_pairs={{0,0},{1,16},{2,2},{3,18},{4,4},{5,20},{6,6},{7,22},{8,12},{9,28},... | collective-permute-start | bytes 3145736 | tf_op jit(solution)/shard_map/ppermute | solution.py:580
  3.2 65.7 %collective-permute-start.1 = (bf16[1024,512]{1,0:T(8,128)(2,1)}, bf16[1024,512]{1,0:T(8,128)(2,1)S(1)}, u32[]{:S(2)}, u32[]{:S(2)}) collective-permute-start(bf16[1024,512]{1,0:T(8,128)(2,1)} %param.11), channel_id=1, source_target_pairs={{0,4},{2,6},{4,12},{6,14},{8,8},{10,10},{12,1},{14,3},{17,21},{19,... | collective-permute-start | bytes 3145736 | tf_op jit(solution)/shard_map/ppermute | solution.py:580
  7.3 61.6 %collective-permute-start.4 = (bf16[1024,512]{1,0:T(8,128)(2,1)}, bf16[1024,512]{1,0:T(8,128)(2,1)}, u32[]{:S(2)}, u32[]{:S(2)}) collective-permute-start(bf16[1024,512]{1,0:T(8,128)(2,1)} %param.11), channel_id=1, source_target_pairs={{0,9},{2,11},{4,0},{6,2},{8,4},{10,6},{12,12},{14,14},{17,24},{19,... | collective-permute-start | bytes 3145736 | tf_op jit(solution)/shard_map/ppermute | solution.py:580
  19.3 12.4 %collective-permute-start = (s32[200,128]{1,0:T(8,128)}, s32[200,128]{1,0:T(8,128)}, u32[]{:S(2)}, u32[]{:S(2)}) collective-permute-start(s32[200,128]{1,0:T(8,128)} %pad_bitcast_fusion), channel_id=1, source_target_pairs={{0,0},{1,16},{2,2},{3,18},{4,4},{5,20},{6,6},{7,22},{8,12},{9,28},... | collective-permute-start | bytes 307208 | tf_op jit(solution)/shard_map/ppermute | solution.py:580
  30.0 24.9 %copy-start.2 = (bf16[1024,512]{1,0:T(8,128)(2,1)}, bf16[1024,512]{1,0:T(8,128)(2,1)S(1)}, u32[]{:S(2)}) copy-start(bf16[1024,512]{1,0:T(8,128)(2,1)S(1)} %collective-permute-done.2.own) | copy-start | bytes 3145732
  30.0 24.9 %collective-permute-start.6 = (bf16[1024,512]{1,0:T(8,128)(2,1)S(1)}, bf16[1024,512]{1,0:T(8,128)(2,1)S(1)}, u32[]{:S(2)}, u32[]{:S(2)}) collective-permute-start(bf16[1024,512]{1,0:T(8,128)(2,1)S(1)} %collective-permute-done.2.own), channel_id=1, source_target_pairs={{0,1},{16,17},{2,3},{18,19},{4,5},{20,21},{6,7},{22,23},{12,13},{2... | collective-permute-start | bytes 3145736 | tf_op jit(solution)/shard_map/ppermute | solution.py:580
  30.0 39.0 %collective-permute-start.5 = (bf16[1024,512]{1,0:T(8,128)(2,1)S(1)}, bf16[1024,512]{1,0:T(8,128)(2,1)}, u32[]{:S(2)}, u32[]{:S(2)}) collective-permute-start(bf16[1024,512]{1,0:T(8,128)(2,1)S(1)} %collective-permute-done.2.own), channel_id=1, source_target_pairs={{16,25},{18,27},{20,16},{22,18},{28,20},{30,22},{24,28},{26,30},{1... | collective-permute-start | bytes 3145736 | tf_op jit(solution)/shard_map/ppermute | solution.py:580
  31.7 37.3 %collective-permute-start.3 = (bf16[1024,512]{1,0:T(8,128)(2,1)S(1)}, bf16[1024,512]{1,0:T(8,128)(2,1)}, u32[]{:S(2)}, u32[]{:S(2)}) collective-permute-start(bf16[1024,512]{1,0:T(8,128)(2,1)S(1)} %collective-permute-done.2.own), channel_id=1, source_target_pairs={{16,20},{18,22},{20,28},{22,30},{28,24},{30,26},{24,17},{26,19},{1... | collective-permute-start | bytes 3145736 | tf_op jit(solution)/shard_map/ppermute | solution.py:580
  86.5 7.7 %collective-permute-start.9 = (bf16[4096,128]{1,0:T(8,128)(2,1)}, bf16[4096,128]{1,0:T(8,128)(2,1)}, u32[]{:S(2)}, u32[]{:S(2)}) collective-permute-start(bf16[4096,128]{1,0:T(8,128)(2,1)} %get-tuple-element.20.own), channel_id=1, source_target_pairs={{0,1},{16,17},{2,3},{18,19},{4,5},{20,21},{6,7},{22,23},{12,13},{2... | collective-permute-start | bytes 3145736 | tf_op jit(solution)/shard_map/ppermute | solution.py:580
  89.7 37.8 %collective-permute-start.10 = (bf16[1024,512]{1,0:T(8,128)(2,1)}, bf16[1024,512]{1,0:T(8,128)(2,1)S(1)}, u32[]{:S(2)}, u32[]{:S(2)}) collective-permute-start(bf16[1024,512]{1,0:T(8,128)(2,1)} %param.19), channel_id=1, source_target_pairs={{0,0},{1,16},{2,2},{3,18},{4,4},{5,20},{6,6},{7,22},{8,12},{9,28},... | collective-permute-start | bytes 3145736 | tf_op jit(solution)/shard_map/ppermute | solution.py:580
  92.1 48.2 %collective-permute-start.8 = (bf16[4096,128]{1,0:T(8,128)(2,1)}, bf16[4096,128]{1,0:T(8,128)(2,1)S(1)}, u32[]{:S(2)}, u32[]{:S(2)}) collective-permute-start(bf16[4096,128]{1,0:T(8,128)(2,1)} %get-tuple-element.20.own), channel_id=1, source_target_pairs={{4,0},{20,16},{6,2},{22,18},{12,4},{28,20},{14,6},{30,22},{8,12},{... | collective-permute-start | bytes 3145736 | tf_op jit(solution)/shard_map/ppermute | solution.py:580
  92.2 48.1 %collective-permute-start.7 = (bf16[4096,128]{1,0:T(8,128)(2,1)}, bf16[4096,128]{1,0:T(8,128)(2,1)S(1)}, u32[]{:S(2)}, u32[]{:S(2)}) collective-permute-start(bf16[4096,128]{1,0:T(8,128)(2,1)} %get-tuple-element.20.own), channel_id=1, source_target_pairs={{9,0},{25,16},{11,2},{27,18},{0,4},{16,20},{2,6},{18,22},{4,12},{2... | collective-permute-start | bytes 3145736 | tf_op jit(solution)/shard_map/ppermute | solution.py:580
  127.5 12.8 %copy-start.1 = (bf16[1024,512]{1,0:T(8,128)(2,1)}, bf16[1024,512]{1,0:T(8,128)(2,1)S(1)}, u32[]{:S(2)}) copy-start(bf16[1024,512]{1,0:T(8,128)(2,1)S(1)} %collective-permute-done.10.cotangent) | copy-start | bytes 3145732
  171.6 22.1 %collective-permute-start.12 = (bf16[4096,128]{1,0:T(8,128)(2,1)}, bf16[4096,128]{1,0:T(8,128)(2,1)S(1)}, u32[]{:S(2)}, u32[]{:S(2)}) collective-permute-start(bf16[4096,128]{1,0:T(8,128)(2,1)} %get-tuple-element.26), channel_id=1, source_target_pairs={{9,0},{25,16},{11,2},{27,18},{0,4},{16,20},{2,6},{18,22},{4,12},{2... | collective-permute-start | bytes 3145736 | tf_op jit(solution)/shard_map/ppermute | solution.py:580
  171.7 22.0 %collective-permute-start.13 = (bf16[4096,128]{1,0:T(8,128)(2,1)}, bf16[4096,128]{1,0:T(8,128)(2,1)S(1)}, u32[]{:S(2)}, u32[]{:S(2)}) collective-permute-start(bf16[4096,128]{1,0:T(8,128)(2,1)} %get-tuple-element.27), channel_id=1, source_target_pairs={{4,0},{20,16},{6,2},{22,18},{12,4},{28,20},{14,6},{30,22},{8,12},{... | collective-permute-start | bytes 3145736 | tf_op jit(solution)/shard_map/ppermute | solution.py:580
  191.7 2.9 %collective-permute-start.14 = (bf16[4096,128]{1,0:T(8,128)(2,1)}, bf16[4096,128]{1,0:T(8,128)(2,1)S(1)}, u32[]{:S(2)}, u32[]{:S(2)}) collective-permute-start(bf16[4096,128]{1,0:T(8,128)(2,1)} %get-tuple-element.28), channel_id=1, source_target_pairs={{0,1},{16,17},{2,3},{18,19},{4,5},{20,21},{6,7},{22,23},{12,13},{2... | collective-permute-start | bytes 3145736 | tf_op jit(solution)/shard_map/ppermute | solution.py:580
  191.7 34.5 %collective-permute-start.11 = (bf16[1024,512]{1,0:T(8,128)(2,1)}, bf16[1024,512]{1,0:T(8,128)(2,1)}, u32[]{:S(2)}, u32[]{:S(2)}) collective-permute-start(bf16[1024,512]{1,0:T(8,128)(2,1)} %get-tuple-element.21), channel_id=1, source_target_pairs={{0,0},{16,1},{2,2},{18,3},{4,4},{20,5},{6,6},{22,7},{12,8},{28,9},... | collective-permute-start | bytes 3145736 | tf_op jit(solution)/shard_map/ppermute | solution.py:580
  203.6 2.4 %collective-permute-start.15 = (f32[72,128]{1,0:T(8,128)}, f32[72,128]{1,0:T(8,128)S(1)}, u32[]{:S(2)}, u32[]{:S(2)}) collective-permute-start(f32[72,128]{1,0:T(8,128)} %last.1), channel_id=1, source_target_pairs={{0,1},{1,0},{2,3},{3,2},{4,5},{5,4},{6,7},{7,6},{8,9},{9,8},{10,11... | collective-permute-start | bytes 110600 | tf_op jit(solution)/shard_map/ppermute | solution.py:580
  206.8 4.0 %collective-permute-start.16 = (f32[72,128]{1,0:T(8,128)S(1)}, f32[72,128]{1,0:T(8,128)S(1)}, u32[]{:S(2)}, u32[]{:S(2)}) collective-permute-start(f32[72,128]{1,0:T(8,128)S(1)} %add.48), channel_id=1, source_target_pairs={{0,2},{1,3},{2,0},{3,1},{4,6},{5,7},{6,4},{7,5},{8,10},{9,11},{10,... | collective-permute-start | bytes 110600 | tf_op jit(solution)/shard_map/ppermute | solution.py:580
  210.7 9.9 %collective-permute-start.17 = (f32[72,128]{1,0:T(8,128)S(1)}, f32[72,128]{1,0:T(8,128)S(1)}, u32[]{:S(2)}, u32[]{:S(2)}) collective-permute-start(f32[72,128]{1,0:T(8,128)S(1)} %add.49), channel_id=1, source_target_pairs={{0,4},{1,5},{2,6},{3,7},{4,0},{5,1},{6,2},{7,3},{8,12},{9,13},{10,... | collective-permute-start | bytes 110600 | tf_op jit(solution)/shard_map/ppermute | solution.py:580
  220.7 4.0 %collective-permute-start.18 = (f32[72,128]{1,0:T(8,128)S(1)}, f32[72,128]{1,0:T(8,128)S(1)}, u32[]{:S(2)}, u32[]{:S(2)}) collective-permute-start(f32[72,128]{1,0:T(8,128)S(1)} %add.50), channel_id=1, source_target_pairs={{0,8},{1,9},{2,10},{3,11},{4,12},{5,13},{6,14},{7,15},{8,0},{9,1},... | collective-permute-start | bytes 110600 | tf_op jit(solution)/shard_map/ppermute | solution.py:580
  224.6 4.9 %collective-permute-start.19 = (f32[72,128]{1,0:T(8,128)S(1)}, f32[72,128]{1,0:T(8,128)S(1)}, u32[]{:S(2)}, u32[]{:S(2)}) collective-permute-start(f32[72,128]{1,0:T(8,128)S(1)} %add.51), channel_id=1, source_target_pairs={{0,16},{1,17},{2,18},{3,19},{4,20},{5,21},{6,22},{7,23},{8,24},{9,... | collective-permute-start | bytes 110600 | tf_op jit(solution)/shard_map/ppermute | solution.py:580
  (8 other events, 8.8 us)
